TPU v7x, 256 devices: a whole 4x4x8 slice. The times are simulated.
256 devices in a mesh: dp: 2 (over y_lo), ctx: 16 (over y_hi, z), head: 8 (over x, core).
Axes of the slice: x: 4, y: 4 (y_hi: 2, y_lo: 2; y = y_hi * 2 + y_lo), z: 8, core: 2. Of those that a mesh axis runs over, the one named last changes fastest.
Arguments:
- queries: bfloat16 [2, 4096, 8192], P('dp', 'ctx', 'head'), may hold values from -45 to 45
- keys: bfloat16 [2, 4096, 1024], P('dp', 'ctx', 'head'), may hold values from -6 to 6
- values: bfloat16 [2, 4096, 1024], P('dp', 'ctx', 'head'), may hold values from -6 to 6
- doc_ids: int32 [2, 4096], P('dp'), may hold values from 0 to 2, never falling along the last dimension, each value on 1 to 3072 neighbouring positions
- inputs: bfloat16 [2, 4096, 8192], P('dp', 'ctx', 'head'), may hold values from -6 to 6
- gate_input: bfloat16 [2, 4096, 8192], P('dp', 'ctx', 'head'), may hold values from -40 to 40
- b_input: bfloat16 [2, 4096, 1024], P('dp', 'ctx', 'head'), may hold values from -0.0625 to 0.0625
- c_input: bfloat16 [2, 4096, 1024], P('dp', 'ctx', 'head'), may hold values from -6 to 6
- dt_raw: float32 [2, 4096, 128], P('dp', 'ctx', 'head'), may hold values from -2 to 2
- dt_bias: float32 [128], P('head'), may hold values from -1 to 1
- decay_log: float32 [128], P('head'), may hold values from -12 to -2
- skip: float32 [128], P('head'), may hold values from 0.5 to 2
- gain: float32 [8192], P('head'), may hold values from 0.5 to 1.5
Outputs:
- teacher_out: bfloat16 [2, 4096, 8192], P('dp', 'ctx', 'head')
- student_out: bfloat16 [2, 4096, 8192], P('dp', 'ctx', 'head')
- grad_gain: float32 [8192], P('head')
- grad_skip: float32 [128], P('head')
Inputs may be any that keep to these rules, and one draw needn't show every extreme that they name: `doc_ids`: three or fewer documents a sequence, numbered from 0 in order; one of them has 3072 positions.
All inputs are finite; a program needn't handle non-finite values.
Results may differ from a plain program's by a relative error of at most 0.012.
Values may be sent and summed in bfloat16 or wider, within the bound.
A program may use at most 64 MiB of HBM per device.

v0:
```python
import jax
import jax.numpy as jnp
from jax import lax
from jax.sharding import Mesh
from jax.sharding import PartitionSpec as P

DH = 128
P_SIZE = 64
N = 128
CTX = ("ctx_0", "ctx_1")
DP_CTX = ("dp", "ctx_0", "ctx_1")


def sent_together(arrays, axis, dim, along):
    both = jnp.concatenate(arrays, axis=along)
    result, at, done = (lax.all_gather(both, axis, axis=dim, tiled=True), 0, [])
    for a in arrays:
        done.append(lax.slice_in_dim(result, at, at + a.shape[along], axis=along))
        at += a.shape[along]
    return tuple(done)


def filled_with(array, identity):
    return jax.tree.map(
        lambda a, e: jnp.broadcast_to(jnp.asarray(e, a.dtype), a.shape), array, identity
    )


def entering(array, axes, combine, identity):
    before = start = filled_with(array, identity)
    so_far = array
    for axis in reversed(axes):
        size, mine = (lax.axis_size(axis), lax.axis_index(axis))
        pieces = jax.tree.map(
            lambda part, kind: lax.all_gather(part.astype(kind), axis),
            so_far,
            (jnp.bfloat16, jnp.bfloat16),
        )
        inside, so_far = (start, start)
        for k in range(size):
            passed = k < mine
            so_far = combine(
                so_far, jax.tree.map(lambda part, own: part[k].astype(own.dtype), pieces, array)
            )
            inside = jax.tree.map(lambda new, old: jnp.where(passed, new, old), so_far, inside)
        before = combine(inside, before)
    return before


def prefix_by_axis(array, axes, combine, identity):
    before = start = filled_with(array, identity)
    so_far = array
    for axis in reversed(axes):
        size, mine = (lax.axis_size(axis), lax.axis_index(axis))
        pieces = jax.tree.map(
            lambda part, kind: lax.all_gather(part.astype(kind), axis),
            so_far,
            jax.tree.map(lambda a: jnp.bfloat16 if a.dtype == jnp.float32 else a.dtype, array),
        )
        inside, so_far = (start, start)
        for k in reversed(range(size)):
            passed = k > mine
            so_far = combine(
                so_far, jax.tree.map(lambda part, own: part[k].astype(own.dtype), pieces, array)
            )
            inside = jax.tree.map(lambda new, old: jnp.where(passed, new, old), so_far, inside)
        before = combine(inside, before)
    return before


def sent_to_all(array, axis):
    copies = jnp.broadcast_to(array, (lax.axis_size(axis), *array.shape))
    return lax.all_to_all(copies, axis, split_axis=0, concat_axis=0, tiled=True)


def over_copies(array, axis):
    everything = sent_to_all(array, axis)
    return jnp.sum(everything, axis=0)


def stored_position(rows, count, stretch, tok_dev):
    device = rows // tok_dev
    offset = rows % tok_dev
    block = jnp.where(offset < stretch, device, 2 * count - 1 - device)
    return block * stretch + offset % stretch


def block_terms(xs, bmat, cmat, dt, rate, docs, prior):
    rows, heads, width = xs.shape
    groups, state = (bmat.shape[1], bmat.shape[2])
    per = heads // groups
    cum = jnp.cumsum(rate, axis=0)
    order = jnp.arange(rows, dtype=jnp.int32)
    allowed = (order[:, None] >= order[None, :]) & (docs[:, None] == docs[None, :])
    gram = jnp.einsum("tgn,sgn->gts", cmat, bmat, preferred_element_type=jnp.float32)
    spans = cum.T[:, :, None] - cum.T[:, None, :]
    fading = jnp.exp(jnp.where(allowed[None], spans, -jnp.inf))
    mixing = (
        fading.reshape(groups, per, rows, rows) * gram[:, None] * dt.T.reshape(groups, per, 1, rows)
    ).astype(jnp.bfloat16)
    grouped = xs.reshape(rows, groups, per, width)
    intra = jnp.einsum(
        "gjts,sgjp->tgjp", mixing, grouped, preferred_element_type=jnp.float32
    ).reshape(rows, heads, width)
    final = cum[-1]
    decay = jnp.where(docs[-1] == prior, jnp.exp(final), 0.0)
    tail = jnp.exp(final[None, :] - cum) * dt * (docs == docs[-1]).astype(jnp.float32)[:, None]
    loaded = (
        tail.reshape(rows, groups, per)[..., None] * bmat[:, :, None, :].astype(jnp.float32)
    ).astype(jnp.bfloat16)
    summary = jnp.einsum(
        "sgjp,sgjn->gjpn", grouped, loaded, preferred_element_type=jnp.float32
    ).reshape(heads, width, state)
    reach = jnp.exp(cum) * (docs == prior).astype(jnp.float32)[:, None]
    return (intra, decay, summary, reach)


def inflow(cmat, state, reach):
    rows, groups, width_n = cmat.shape
    heads = state.shape[0]
    per = heads // groups
    grouped = state.reshape(groups, per, state.shape[1], width_n)
    flow = jnp.einsum("tgn,gjpn->tgjp", cmat.astype(jnp.float32), grouped)
    return flow.reshape(rows, heads, state.shape[1]) * reach[:, :, None]


def combine(earlier, later):
    return (earlier[0] * later[0], later[0][:, None, None] * earlier[1] + later[1])


def gated_norm(mixed, xs, gate, skip, gain, groups):
    rows, heads, width = mixed.shape
    values_out = mixed + skip[None, :, None] * xs.astype(jnp.float32)
    gated = values_out.reshape(rows, heads * width) * jax.nn.silu(gate.astype(jnp.float32))
    gated = gated.reshape(rows, groups, -1)
    normed = gated * lax.rsqrt(jnp.mean(gated * gated, axis=2, keepdims=True) + 1e-05)
    return normed.reshape(rows, heads * width) * gain


def body(
    queries,
    keys,
    values,
    doc_ids,
    inputs,
    gate_input,
    b_input,
    c_input,
    dt_raw,
    dt_bias,
    decay_log,
    skip,
    gain,
):
    count = lax.axis_size(CTX)
    index = lax.axis_index(CTX)
    tok_dev = queries.shape[1]
    stretch = tok_dev // 2
    kv_dev = keys.shape[2] // DH
    per_kv = queries.shape[2] // keys.shape[2]
    docs = doc_ids[0]
    local_rows = index * tok_dev + jnp.arange(tok_dev, dtype=jnp.int32)
    local_pos = stored_position(local_rows, count, stretch, tok_dev)
    local_docs = jnp.take(docs, local_pos)
    query_block = queries[0].reshape(tok_dev, kv_dev, per_kv, DH)
    scale = 1.0 / jnp.sqrt(jnp.float32(DH))
    start_state = (
        jnp.full((tok_dev, kv_dev, per_kv), -1e30, jnp.float32),
        jnp.zeros((tok_dev, kv_dev, per_kv), jnp.float32),
        jnp.zeros((tok_dev, kv_dev, per_kv, DH), jnp.float32),
    )
    carry = start_state
    key_piece, value_piece = sent_together((keys, values), CTX, 1, 0)
    size = key_piece.shape[1]
    span = 512
    key_tiles = key_piece[0].reshape(size // span, span, kv_dev, DH)
    value_tiles = value_piece[0].reshape(size // span, span, kv_dev, DH)
    key_pos = stored_position(jnp.arange(size, dtype=jnp.int32), count, stretch, tok_dev)
    key_docs = jnp.take(docs, key_pos).reshape(size // span, span)
    key_pos = key_pos.reshape(size // span, span)

    def inner(state, items):
        top, total, summed = state
        key_now, value_now, pos_now, doc_now = items
        scores = (
            jnp.einsum("tkgd,skd->tkgs", query_block, key_now, preferred_element_type=jnp.float32)
            * scale
        )
        allowed = (
            (local_pos[:, None] >= pos_now[None, :]) & (local_docs[:, None] == doc_now[None, :])
        )[:, None, None, :]
        new_top = jnp.maximum(top, jnp.max(jnp.where(allowed, scores, -1e30), axis=3))
        weights = jnp.where(allowed, jnp.exp(scores - new_top[..., None]), 0.0)
        factor = jnp.exp(top - new_top)
        total = total * factor + jnp.sum(weights, axis=3)
        summed = summed * factor[..., None] + jnp.einsum(
            "tkgs,skd->tkgd",
            weights.astype(jnp.bfloat16),
            value_now,
            preferred_element_type=jnp.float32,
        )
        return ((new_top, total, summed), None)

    carry, _ = lax.scan(inner, carry, (key_tiles, value_tiles, key_pos, key_docs))
    top, total, summed = carry
    teacher = (
        (summed / total[..., None]).reshape(1, tok_dev, kv_dev * per_kv * DH).astype(jnp.bfloat16)
    )
    heads = inputs.shape[2] // P_SIZE
    groups = b_input.shape[2] // N
    dt = jax.nn.softplus(dt_raw[0] + dt_bias)
    rate = -dt * jnp.exp(decay_log)
    xs = inputs[0].reshape(tok_dev, heads, P_SIZE)
    bmat = b_input[0].reshape(tok_dev, groups, N)
    cmat = c_input[0].reshape(tok_dev, groups, N)

    def prior_doc(first):
        return jnp.where(first > 0, jnp.take(docs, jnp.maximum(first - 1, 0)), -1)

    front_first = index * stretch
    back_first = (2 * count - 1 - index) * stretch
    intra_f, decay_f, summ_f, reach_f = block_terms(
        xs[:stretch],
        bmat[:stretch],
        cmat[:stretch],
        dt[:stretch],
        rate[:stretch],
        local_docs[:stretch],
        prior_doc(front_first),
    )
    intra_b, decay_b, summ_b, reach_b = block_terms(
        xs[stretch:],
        bmat[stretch:],
        cmat[stretch:],
        dt[stretch:],
        rate[stretch:],
        local_docs[stretch:],
        prior_doc(back_first),
    )
    identity = (jnp.ones_like(decay_f), jnp.zeros_like(summ_f))
    before_front = entering((decay_f, summ_f), CTX, combine, identity)
    through_front = combine(before_front, (decay_f, summ_f))
    last = count - 1
    is_last = index == last
    joined = combine(through_front, (decay_b, summ_b))
    sent = (jnp.where(is_last, joined[0], decay_b), jnp.where(is_last, joined[1], summ_b))
    after = prefix_by_axis(sent, CTX, combine, identity)
    back_state = jnp.where(is_last, through_front[1], after[1])
    mixed_front = intra_f + inflow(cmat[:stretch], before_front[1], reach_f)
    mixed_back = intra_b + inflow(cmat[stretch:], back_state, reach_b)
    mixed = jnp.concatenate([mixed_front, mixed_back], axis=0)
    target = teacher[0].astype(jnp.float32)
    loss_scale = 1.0 / (lax.axis_size("dp") * count * tok_dev)

    def local_loss(gain_part, skip_part):
        normed = gated_norm(mixed, xs, gate_input[0], skip_part, gain_part, groups)
        diff = normed - target
        return (jnp.sum(diff * diff) * loss_scale, normed)

    (grad_gain, grad_skip), normed = jax.grad(local_loss, argnums=(0, 1), has_aux=True)(gain, skip)
    summed_grads = (over_copies(grad_gain, DP_CTX), over_copies(grad_skip, DP_CTX))
    student = normed.astype(jnp.bfloat16).reshape(1, tok_dev, heads * P_SIZE)
    return (teacher, student, summed_grads[0], summed_grads[1])


def solution(mesh):
    split = Mesh(
        mesh.devices.reshape(mesh.shape["dp"], 2, 8, mesh.shape["head"]),
        ("dp", "ctx_0", "ctx_1", "head"),
    )
    placed = (
        P("dp", CTX, "head"),
        P("dp", CTX, "head"),
        P("dp", CTX, "head"),
        P("dp", None),
        P("dp", CTX, "head"),
        P("dp", CTX, "head"),
        P("dp", CTX, "head"),
        P("dp", CTX, "head"),
        P("dp", CTX, "head"),
        P("head"),
        P("head"),
        P("head"),
        P("head"),
    )
    return jax.shard_map(
        body,
        mesh=split,
        in_specs=placed,
        out_specs=(P("dp", CTX, "head"), P("dp", CTX, "head"), P("head"), P("head")),
        check_vma=False,
    )
```

profile of v0, /device:TPU:4, one launch (start us, length us, event | category | flops | bytes accessed | tf_op | source)
XLA Modules:
  0.0 258.4 jit_solution(13145956909542441902)
XLA Ops:
  7.3 1.3 constant_dynamic-slice_fusion.2
  9.3 2.0 gather_fusion
  13.9 1.4 bitcast_convert_fusion
  17.2 1.3 compare_convert_fusion.2
  18.7 1.8 fusion.321
  20.7 1.4 fusion.325
  24.2 19.3 %all-gather.2 = bf16[8,1,16]{2,1,0:T(2,128)(2,1)S(1)} all-gather(bf16[1,1,16]{2,1,0:T(2,128)(2,1)S(1)} %get-tuple-element.235), channel_id=1, replica_groups=mesh['dp'=2,'ctx_0'=2,'ctx_1'=8,'head'=8] {'ctx_1'}, dimensions={0}, use_global_device_ids=true | all-gather | bytes 288 | tf_op jit(solution)/shard_map/all_gather | solution.py:35
  43.5 5.7 %all-gather.3 = bf16[2,1,16]{2,1,0:T(2,128)(2,1)S(1)} all-gather(bf16[1,1,16]{2,1,0:T(2,128)(2,1)S(1)} %get-tuple-element.213), channel_id=1, replica_groups=mesh['dp'=2,'ctx_0'=2,'ctx_1'=8,'head'=8] {'ctx_0'}, dimensions={0}, use_global_device_ids=true | all-gather | bytes 96 | tf_op jit(solution)/shard_map/all_gather | solution.py:35
  52.0 23.0 %gather_fusion.1 = s32[4096]{0:T(1024)S(1)} fusion(s32[4096]{0:T(1024)S(1)} %bitcast.701, s32[4096]{0:T(1024)S(1)} %broadcast_clamp_fusion), kind=kCustom, calls=%fused_computation.1 | custom fusion | bytes 49152 | tf_op jit(solution)/shard_map/jit(_take)/gather | solution.py:179
  76.2 13.3 %all-gather.4 = bf16[8,1,16]{2,1,0:T(2,128)(2,1)S(1)} all-gather(bf16[1,1,16]{2,1,0:T(2,128)(2,1)S(1)} %fusion.288), channel_id=1, replica_groups=mesh['dp'=2,'ctx_0'=2,'ctx_1'=8,'head'=8] {'ctx_1'}, dimensions={0}, use_global_device_ids=true | all-gather | bytes 288 | tf_op jit(solution)/shard_map/all_gather | solution.py:56
  90.2 5.7 %all-gather.5 = bf16[2,1,16]{2,1,0:T(2,128)(2,1)S(1)} all-gather(bf16[1,1,16]{2,1,0:T(2,128)(2,1)S(1)} %fusion.297), channel_id=1, replica_groups=mesh['dp'=2,'ctx_0'=2,'ctx_1'=8,'head'=8] {'ctx_0'}, dimensions={0}, use_global_device_ids=true | all-gather | bytes 96 | tf_op jit(solution)/shard_map/all_gather | solution.py:56
  100.7 1.2 copy.108
  102.2 1.8 copy.123
  104.0 1.3 broadcast_select_fusion.20
  105.3 1.2 fusion.294
  106.5 1.3 fusion.311
  108.9 1.3 broadcast_multiply_fusion
  111.7 1.4 fusion.274
  113.1 0.9 fusion.259
  114.0 0.9 fusion.263
  114.9 1.3 fusion.85
  116.4 2.5 fusion.86
  118.9 2.1 fusion.175
  121.0 13.2 %all_gather.44 = bf16[2,16,64,128]{3,2,1,0:T(8,128)(2,1)S(1)} all-gather(bf16[1,16,64,128]{3,2,1,0:T(8,128)(2,1)S(1)} %fusion.175), channel_id=1, replica_groups=mesh['dp'=2,'ctx_0'=2,'ctx_1'=8,'head'=8] {'ctx_0'}, dimensions={0}, use_global_device_ids=true | all-gather | bytes 786432 | tf_op jit(solution)/shard_map/all_gather | solution.py:35
  134.5 2.6 fusion.112
  138.9 1.5 fusion.107
  140.4 1.2 fusion.78
  141.7 1.3 add.603
  143.0 12.5 %all-gather.10.cloned.1.call-done = bf16[2,4096,128]{2,1,0:T(8,128)(2,1)} async-done(((bf16[2,256,128]{2,1,0:T(8,128)(2,1)}), bf16[2,4096,128]{2,1,0:T(8,128)(2,1)}) %all-gather.10.cloned.1.call-update) | async-done | bytes 2097168 | tf_op jit(solution)/shard_map/all_gather | solution.py:16
  155.5 3.0 %fusion.320 = (bf16[1,4096,128]{2,1,0:T(8,128)(2,1)}, bf16[1,4096,128]{2,1,0:T(8,128)(2,1)}) fusion(bf16[2,4096,128]{2,1,0:T(8,128)(2,1)} %all-gather.10.cloned.1.call-done), kind=kLoop, calls=%fused_computation.526 | loop fusion | bytes 4194304 | tf_op jit(solution)/shard_map/slice | solution.py:18
  158.6 45.3 %while.17 = (s32[]{:T(128)}, f32[256,1,8]{0,2,1:T(8,128)S(1)}, f32[256,1,8]{0,2,1:T(8,128)S(1)}, f32[256,1,8,128]{0,3,2,1:T(8,128)S(1)}, s32[8,512]{1,0:T(8,128)...) while((s32[]{:T(128)}, f32[256,1,8]{0,2,1:T(8,128)S(1)}, ...), condition=%wide.region_3.4_spmd.clone, body=%wide.region_0.3_spmd.clone.sunk | while | flops 549606400 | bytes 16137377 | solution.py:204
  159.6 1.7 fusion.340
  162.2 2.0 fusion.343
  165.3 1.7 fusion.340
  167.0 0.9 fusion.342
  167.9 2.0 fusion.343
  171.0 1.7 fusion.340
  172.7 0.9 fusion.342
  173.5 2.0 fusion.343
  176.6 1.7 fusion.340
  178.3 0.9 fusion.342
  179.2 2.0 fusion.343
  182.3 1.7 fusion.340
  184.0 0.9 fusion.342
  184.9 2.0 fusion.343
  187.9 1.7 fusion.340
  190.5 2.0 fusion.343
  193.6 1.7 fusion.340
  196.2 2.0 fusion.343
  199.3 1.7 fusion.340
  201.0 0.9 fusion.342
  201.8 2.0 fusion.343
  204.0 2.1 fusion.191
  206.1 8.7 %all_gather.49 = bf16[2,16,64,128]{3,2,1,0:T(8,128)(2,1)S(1)} all-gather(bf16[1,16,64,128]{3,2,1,0:T(8,128)(2,1)S(1)} %fusion.191), channel_id=1, replica_groups=mesh['dp'=2,'ctx_0'=2,'ctx_1'=8,'head'=8] {'ctx_0'}, dimensions={0}, use_global_device_ids=true | all-gather | bytes 786432 | tf_op jit(solution)/shard_map/all_gather | solution.py:56
  214.8 2.4 fusion.96
  219.1 1.3 fusion.44
  221.3 5.1 %all-to-all-start.1 = ((f32[32,1,16]{2,1,0:T(1,128)}), f32[32,1,16]{2,1,0:T(1,128)S(1)}, u32[]{:S(2)}, u32[]{:S(2)}) async-start(f32[32,1,16]{2,1,0:T(1,128)} %broadcast_in_dim.104), calls=%async_computation.1 | async-start | bytes 32768 | tf_op jit(solution)/shard_map/all_to_all | solution.py:73
  226.4 2.0 fusion.77
  228.4 1.1 fusion.153
  229.5 6.7 %all-to-all-done.1 = f32[32,1,16]{2,1,0:T(1,128)S(1)} async-done(((f32[32,1,16]{2,1,0:T(1,128)}), f32[32,1,16]{2,1,0:T(1,128)S(1)}, u32[]{:S(2)}, u32[]{:S(2)}) %all-to-all-start.1) | async-done | bytes 2080 | tf_op jit(solution)/shard_map/all_to_all | solution.py:73
  236.9 3.9 %all-to-all-start = ((f32[32,1,1024]{2,1,0:T(1,128)}), f32[32,1,1024]{2,1,0:T(1,128)S(1)}, u32[]{:S(2)}, u32[]{:S(2)}) async-start(f32[32,1,1024]{2,1,0:T(1,128)} %broadcast_in_dim.102), calls=%async_computation | async-start | bytes 262144 | tf_op jit(solution)/shard_map/all_to_all | solution.py:73
  241.3 1.0 copy.130
  242.3 1.0 copy.132
  243.9 7.4 %all-to-all-done = f32[32,1,1024]{2,1,0:T(1,128)S(1)} async-done(((f32[32,1,1024]{2,1,0:T(1,128)}), f32[32,1,1024]{2,1,0:T(1,128)S(1)}, u32[]{:S(2)}, u32[]{:S(2)}) %all-to-all-start) | async-done | bytes 131104 | tf_op jit(solution)/shard_map/all_to_all | solution.py:73
  (250 shorter events, 34.8 us)
Async XLA Ops:
  7.2 44.8 %copy-start = (s32[1,4096]{1,0:T(1,128)S(1)}, s32[1,4096]{1,0:T(1,128)}, u32[]{:S(2)}) copy-start(s32[1,4096]{1,0:T(1,128)} %param.18) | copy-start | bytes 49156
  7.2 43.8 %copy-start.8 = (bf16[1,256,1024]{2,1,0:T(8,128)(2,1)S(1)}, bf16[1,256,1024]{2,1,0:T(8,128)(2,1)}, u32[]{:S(2)}) copy-start(bf16[1,256,1024]{2,1,0:T(8,128)(2,1)} %param.19) | copy-start | bytes 1572868
  7.2 15.0 %copy-start.20 = (bf16[1,256,128]{2,1,0:T(8,128)(2,1)S(1)}, bf16[1,256,128]{2,1,0:T(8,128)(2,1)}, u32[]{:S(2)}) copy-start(bf16[1,256,128]{2,1,0:T(8,128)(2,1)} %param.17) | copy-start | bytes 196612
  7.2 15.0 %copy-start.21 = (bf16[1,256,128]{2,1,0:T(8,128)(2,1)S(1)}, bf16[1,256,128]{2,1,0:T(8,128)(2,1)}, u32[]{:S(2)}) copy-start(bf16[1,256,128]{2,1,0:T(8,128)(2,1)} %param.16) | copy-start | bytes 196612
  7.2 44.0 %copy-start.53 = (f32[16]{0:T(128)S(1)}, f32[16]{0:T(128)}, u32[]{:S(2)}) copy-start(f32[16]{0:T(128)} %param.26) | copy-start | bytes 196
  7.2 111.7 %all-gather.12.cloned.1.call-start = ((), (), s32[]{:S(2)}) async-start(), calls=%async_computation.3 | async-start | bytes 2359296 | tf_op jit(solution)/shard_map/all_gather | solution.py:35
  11.3 12.8 %copy-start.15 = (s32[256]{0:T(256)}, s32[256]{0:T(256)S(1)}, u32[]{:S(2)}) copy-start(s32[256]{0:T(256)S(1)} %and_select_fusion.10) | copy-start | bytes 3076
  22.1 133.3 %all-gather.10.cloned.1.call-start = ((), (), s32[]{:S(2)}) async-start(), calls=%async_computation.2 | async-start | bytes 2228224 | tf_op jit(solution)/shard_map/all_gather | solution.py:16
  22.9 181.0 %all-gather.14.cloned.1.call-start = ((), (), s32[]{:S(2)}) async-start(), calls=%async_computation.4 | async-start | bytes 2359296 | tf_op jit(solution)/shard_map/all_gather | solution.py:56
  52.0 48.5 %copy-start.10 = (bf16[1,256,1024]{2,1,0:T(8,128)(2,1)S(1)}, bf16[1,256,1024]{2,1,0:T(8,128)(2,1)}, u32[]{:S(2)}) copy-start(bf16[1,256,1024]{2,1,0:T(8,128)(2,1)} %param.20) | copy-start | bytes 1572868
  89.5 10.3 %copy-start.24 = (bf16[8,1,16]{2,1,0:T(2,128)(2,1)}, bf16[8,1,16]{2,1,0:T(2,128)(2,1)S(1)}, u32[]{:S(2)}) copy-start(bf16[8,1,16]{2,1,0:T(2,128)(2,1)S(1)} %all-gather.4) | copy-start | bytes 772
  95.9 3.9 %copy-start.60 = (bf16[2,1,16]{2,1,0:T(2,128)(2,1)}, bf16[2,1,16]{2,1,0:T(2,128)(2,1)S(1)}, u32[]{:S(2)}) copy-start(bf16[2,1,16]{2,1,0:T(2,128)(2,1)S(1)} %all-gather.5) | copy-start | bytes 196
  116.3 21.7 %copy-start.6 = (f32[16,128,64]{1,2,0:T(8,128)}, f32[16,128,64]{1,2,0:T(8,128)S(1)}, u32[]{:S(2)}) copy-start(f32[16,128,64]{1,2,0:T(8,128)S(1)} %fusion.85) | copy-start | bytes 1572868
  116.3 18.0 %copy-start.22 = (bf16[1,256,128]{2,1,0:T(8,128)(2,1)S(1)}, bf16[1,256,128]{2,1,0:T(8,128)(2,1)}, u32[]{:S(2)}) copy-start(bf16[1,256,128]{2,1,0:T(8,128)(2,1)} %param.22) | copy-start | bytes 196612
  116.3 18.0 %copy-start.27 = (f32[16]{0:T(128)S(1)}, f32[16]{0:T(128)}, u32[]{:S(2)}) copy-start(f32[16]{0:T(128)} %get-tuple-element.250) | copy-start | bytes 196
  116.3 18.0 %copy-start.29 = (f32[16]{0:T(128)S(1)}, f32[16]{0:T(128)}, u32[]{:S(2)}) copy-start(f32[16]{0:T(128)} %get-tuple-element.251) | copy-start | bytes 196
  116.3 18.0 %copy-start.31 = (f32[16]{0:T(128)S(1)}, f32[16]{0:T(128)}, u32[]{:S(2)}) copy-start(f32[16]{0:T(128)} %get-tuple-element.252) | copy-start | bytes 196
  116.3 18.0 %copy-start.33 = (f32[16]{0:T(128)S(1)}, f32[16]{0:T(128)}, u32[]{:S(2)}) copy-start(f32[16]{0:T(128)} %get-tuple-element.253) | copy-start | bytes 196
  116.3 18.0 %copy-start.35 = (f32[16]{0:T(128)S(1)}, f32[16]{0:T(128)}, u32[]{:S(2)}) copy-start(f32[16]{0:T(128)} %get-tuple-element.254) | copy-start | bytes 196
  116.3 18.0 %copy-start.37 = (f32[16]{0:T(128)S(1)}, f32[16]{0:T(128)}, u32[]{:S(2)}) copy-start(f32[16]{0:T(128)} %get-tuple-element.255) | copy-start | bytes 196
  116.3 18.0 %copy-start.39 = (f32[16]{0:T(128)S(1)}, f32[16]{0:T(128)}, u32[]{:S(2)}) copy-start(f32[16]{0:T(128)} %get-tuple-element.256) | copy-start | bytes 196
  116.4 18.0 %copy-start.41 = (f32[16]{0:T(128)S(1)}, f32[16]{0:T(128)}, u32[]{:S(2)}) copy-start(f32[16]{0:T(128)} %get-tuple-element.249) | copy-start | bytes 196
  116.4 18.0 %copy-start.51 = (f32[16]{0:T(128)S(1)}, f32[16]{0:T(128)}, u32[]{:S(2)}) copy-start(f32[16]{0:T(128)} %get-tuple-element.248) | copy-start | bytes 196
  116.4 18.0 %copy-start.55 = (f32[16]{0:T(128)S(1)}, f32[16]{0:T(128)}, u32[]{:S(2)}) copy-start(f32[16]{0:T(128)} %fusion.304) | copy-start | bytes 196
  116.4 18.0 %copy-start.57 = (f32[16]{0:T(128)S(1)}, f32[16]{0:T(128)}, u32[]{:S(2)}) copy-start(f32[16]{0:T(128)} %multiply_bitcast_fusion) | copy-start | bytes 196
  121.0 16.0 %copy-start.18 = (f32[128,16]{0,1:T(8,128)S(1)}, f32[128,16]{0,1:T(8,128)}, u32[]{:S(2)}) copy-start(f32[128,16]{0,1:T(8,128)} %copy.119) | copy-start | bytes 24580
  134.3 4.4 %copy-start.1 = (bf16[128,64,128]{2,1,0:T(8,128)(2,1)S(1)}, bf16[128,64,128]{2,1,0:T(8,128)(2,1)}, u32[]{:S(2)}) copy-start(bf16[128,64,128]{2,1,0:T(8,128)(2,1)} %all-gather.12.cloned.1.call-done) | copy-start | bytes 6291460
  134.4 4.4 %copy-start.9 = (f32[16,64,128]{2,1,0:T(8,128)S(1)}, f32[16,64,128]{2,1,0:T(8,128)}, u32[]{:S(2)}) copy-start(f32[16,64,128]{2,1,0:T(8,128)} %get-tuple-element.266) | copy-start | bytes 1572868
  134.4 4.4 %copy-start.28 = (f32[16]{0:T(128)S(1)}, f32[16]{0:T(128)}, u32[]{:S(2)}) copy-start(f32[16]{0:T(128)} %get-tuple-element.250) | copy-start | bytes 196
  134.4 4.4 %copy-start.30 = (f32[16]{0:T(128)S(1)}, f32[16]{0:T(128)}, u32[]{:S(2)}) copy-start(f32[16]{0:T(128)} %get-tuple-element.251) | copy-start | bytes 196
  134.4 4.4 %copy-start.32 = (f32[16]{0:T(128)S(1)}, f32[16]{0:T(128)}, u32[]{:S(2)}) copy-start(f32[16]{0:T(128)} %get-tuple-element.252) | copy-start | bytes 196
  134.4 4.4 %copy-start.34 = (f32[16]{0:T(128)S(1)}, f32[16]{0:T(128)}, u32[]{:S(2)}) copy-start(f32[16]{0:T(128)} %get-tuple-element.253) | copy-start | bytes 196
  134.4 4.4 %copy-start.36 = (f32[16]{0:T(128)S(1)}, f32[16]{0:T(128)}, u32[]{:S(2)}) copy-start(f32[16]{0:T(128)} %get-tuple-element.254) | copy-start | bytes 196
  134.4 4.4 %copy-start.38 = (f32[16]{0:T(128)S(1)}, f32[16]{0:T(128)}, u32[]{:S(2)}) copy-start(f32[16]{0:T(128)} %get-tuple-element.255) | copy-start | bytes 196
  134.4 4.4 %copy-start.40 = (f32[16]{0:T(128)S(1)}, f32[16]{0:T(128)}, u32[]{:S(2)}) copy-start(f32[16]{0:T(128)} %get-tuple-element.256) | copy-start | bytes 196
  134.4 4.4 %copy-start.42 = (f32[16]{0:T(128)S(1)}, f32[16]{0:T(128)}, u32[]{:S(2)}) copy-start(f32[16]{0:T(128)} %get-tuple-element.249) | copy-start | bytes 196
  134.4 4.4 %copy-start.52 = (f32[16]{0:T(128)S(1)}, f32[16]{0:T(128)}, u32[]{:S(2)}) copy-start(f32[16]{0:T(128)} %get-tuple-element.248) | copy-start | bytes 196
  134.5 4.4 %copy-start.56 = (f32[16]{0:T(128)S(1)}, f32[16]{0:T(128)}, u32[]{:S(2)}) copy-start(f32[16]{0:T(128)} %fusion.304) | copy-start | bytes 196
  134.5 4.4 %copy-start.58 = (f32[16]{0:T(128)S(1)}, f32[16]{0:T(128)}, u32[]{:S(2)}) copy-start(f32[16]{0:T(128)} %multiply_bitcast_fusion) | copy-start | bytes 196
  134.5 4.4 %copy-start.59 = (f32[16]{0:T(128)S(1)}, f32[16]{0:T(128)}, u32[]{:S(2)}) copy-start(f32[16]{0:T(128)} %broadcast_select_fusion.21) | copy-start | bytes 196
  137.1 3.3 %copy-start.12 = (bf16[1,128,1024]{1,2,0:T(8,128)(2,1)S(1)}, bf16[1,128,1024]{1,2,0:T(8,128)(2,1)}, u32[]{:S(2)}) copy-start(bf16[1,128,1024]{1,2,0:T(8,128)(2,1)} %copy.123) | copy-start | bytes 786436
  137.1 3.3 %copy-start.19 = (f32[128,128]{1,0:T(8,128)S(1)}, f32[128,128]{1,0:T(8,128)}, u32[]{:S(2)}) copy-start(f32[128,128]{1,0:T(8,128)} %get-tuple-element.233) | copy-start | bytes 196612
  137.1 3.3 %copy-start.26 = (f32[128,16]{0,1:T(8,128)S(1)}, f32[128,16]{0,1:T(8,128)}, u32[]{:S(2)}) copy-start(f32[128,16]{0,1:T(8,128)} %copy.124) | copy-start | bytes 24580
  137.1 3.3 %copy-start.61 = (f32[16]{0:T(128)S(1)}, f32[16]{0:T(128)}, u32[]{:S(2)}) copy-start(f32[16]{0:T(128)} %broadcast_select_fusion.4) | copy-start | bytes 196
  140.4 18.2 %copy-start.16 = (s32[256]{0:T(256)S(1)}, s32[256]{0:T(256)}, u32[]{:S(2)}) copy-start(s32[256]{0:T(256)} %copy-done.15) | copy-start | bytes 3076
  158.5 45.4 %copy-start.43 = (f32[16]{0:T(128)S(1)}, f32[16]{0:T(128)}, u32[]{:S(2)}) copy-start(f32[16]{0:T(128)} %get-tuple-element.241) | copy-start | bytes 196
  158.5 45.4 %copy-start.44 = (f32[16]{0:T(128)S(1)}, f32[16]{0:T(128)}, u32[]{:S(2)}) copy-start(f32[16]{0:T(128)} %get-tuple-element.242) | copy-start | bytes 196
  158.5 45.4 %copy-start.45 = (f32[16]{0:T(128)S(1)}, f32[16]{0:T(128)}, u32[]{:S(2)}) copy-start(f32[16]{0:T(128)} %get-tuple-element.243) | copy-start | bytes 196
  158.6 45.4 %copy-start.46 = (f32[16]{0:T(128)S(1)}, f32[16]{0:T(128)}, u32[]{:S(2)}) copy-start(f32[16]{0:T(128)} %get-tuple-element.244) | copy-start | bytes 196
  158.6 45.4 %copy-start.47 = (f32[16]{0:T(128)S(1)}, f32[16]{0:T(128)}, u32[]{:S(2)}) copy-start(f32[16]{0:T(128)} %get-tuple-element.245) | copy-start | bytes 196
  158.6 45.4 %copy-start.48 = (f32[16]{0:T(128)S(1)}, f32[16]{0:T(128)}, u32[]{:S(2)}) copy-start(f32[16]{0:T(128)} %get-tuple-element.246) | copy-start | bytes 196
  158.6 45.4 %copy-start.49 = (f32[16]{0:T(128)S(1)}, f32[16]{0:T(128)}, u32[]{:S(2)}) copy-start(f32[16]{0:T(128)} %get-tuple-element.247) | copy-start | bytes 196
  158.6 45.4 %copy-start.50 = (f32[16]{0:T(128)S(1)}, f32[16]{0:T(128)}, u32[]{:S(2)}) copy-start(f32[16]{0:T(128)} %get-tuple-element.240) | copy-start | bytes 196
  158.6 56.2 %copy-start.23 = (bf16[1,256,128]{2,1,0:T(8,128)(2,1)S(1)}, bf16[1,256,128]{2,1,0:T(8,128)(2,1)}, u32[]{:S(2)}) copy-start(bf16[1,256,128]{2,1,0:T(8,128)(2,1)} %param.22) | copy-start | bytes 196612
  158.6 56.2 %copy-start.54 = (f32[16]{0:T(128)S(1)}, f32[16]{0:T(128)}, u32[]{:S(2)}) copy-start(f32[16]{0:T(128)} %get-tuple-element.239) | copy-start | bytes 196
  158.6 56.2 %copy-start.62 = (f32[16]{0:T(128)S(1)}, f32[16]{0:T(128)}, u32[]{:S(2)}) copy-start(f32[16]{0:T(128)} %fusion.295) | copy-start | bytes 196
  158.6 56.2 %copy-start.63 = (f32[16]{0:T(128)S(1)}, f32[16]{0:T(128)}, u32[]{:S(2)}) copy-start(f32[16]{0:T(128)} %fusion.294) | copy-start | bytes 196
  206.1 11.2 %copy-start.17 = (f32[128,16]{0,1:T(8,128)S(1)}, f32[128,16]{0,1:T(8,128)}, u32[]{:S(2)}) copy-start(f32[128,16]{0,1:T(8,128)} %copy.125) | copy-start | bytes 24580
  206.1 11.2 %copy-start.4 = (f32[16,128,64]{1,2,0:T(8,128)S(1)}, f32[16,128,64]{1,2,0:T(8,128)}, u32[]{:S(2)}) copy-start(f32[16,128,64]{1,2,0:T(8,128)} %fusion.86) | copy-start | bytes 1572868
  214.8 3.2 %copy-start.14 = (f32[1024]{0:T(1024)S(1)}, f32[1024]{0:T(1024)}, u32[]{:S(2)}) copy-start(f32[1024]{0:T(1024)} %mul.1223) | copy-start | bytes 12292
  219.0 9.4 %copy-start.5 = (f32[16,128,64]{1,2,0:T(8,128)S(1)}, f32[16,128,64]{1,2,0:T(8,128)}, u32[]{:S(2)}) copy-start(f32[16,128,64]{1,2,0:T(8,128)} %fusion.86) | copy-start | bytes 1572868
  219.1 21.7 %copy-start.3 = (f32[1,128,1024]{1,2,0:T(8,128)S(1)}, f32[1,128,1024]{1,2,0:T(8,128)}, u32[]{:S(2)}) copy-start(f32[1,128,1024]{1,2,0:T(8,128)} %fusion.161) | copy-start | bytes 1572868
  221.3 15.0 %all-to-all-start.1 = ((f32[32,1,16]{2,1,0:T(1,128)}), f32[32,1,16]{2,1,0:T(1,128)S(1)}, u32[]{:S(2)}, u32[]{:S(2)}) async-start(f32[32,1,16]{2,1,0:T(1,128)} %broadcast_in_dim.104), calls=%async_computation.1 | async-start | bytes 32768 | tf_op jit(solution)/shard_map/all_to_all | solution.py:73
  236.9 14.3 %all-to-all-start = ((f32[32,1,1024]{2,1,0:T(1,128)}), f32[32,1,1024]{2,1,0:T(1,128)S(1)}, u32[]{:S(2)}, u32[]{:S(2)}) async-start(f32[32,1,1024]{2,1,0:T(1,128)} %broadcast_in_dim.102), calls=%async_computation | async-start | bytes 262144 | tf_op jit(solution)/shard_map/all_to_all | solution.py:73
  (5 other events, 6.3 us)
Sparse Core Ops, SparseCore 0:
  22.3 43.6 all-gather.11
  68.5 86.9 all-gather.9
  157.3 37.4 all-gather.13
where the time goes:
time: 261 us; the launch traced here: 258 us
  blocking collectives  65.9 us (25%)
  local copies, waits for them, and re-layouts  54 us (21%)
  matrix products  43.1 us (17%)
  other arithmetic  41.6 us (16%)
  waiting for transfers between devices  26.7 us (10%)
  between operations  17.5 us (7%)
  starting transfers between devices  9.11 us (3%)
    all_gather x3, blocking collectives, entering(): lax.all_gather(part.astype(kind), axis)  38.2 us
    all_gather x3, blocking collectives, prefix_by_axis(): lax.all_gather(part.astype(kind), axis)  27.7 us
    gather x2, local copies, waits for them, and re-layouts, body(): key_docs = jnp.take(docs, key_pos).reshape(size // span, span)  23.6 us
    dot_general x8, matrix products, inner(): jnp.einsum('tkgs,skd->tkgd', weights.astype(jnp.bfloat16), value_now, pre...  16.3 us
    all_to_all x2, waiting for transfers between devices, sent_to_all(): return lax.all_to_all(copies, axis, split_axis=0, concat_axis=0, tiled=True)  14.1 us
    dot_general x8, matrix products, inner(): jnp.einsum('tkgd,skd->tkgs', query_block, key_now, preferred_element_type...  13.5 us
    all_gather x1, waiting for transfers between devices, sent_together(): result, at, done = (lax.all_gather(both, axis, axis=dim, tiled=True), 0, [])  12.5 us
    all_to_all x2, starting transfers between devices, sent_to_all(): return lax.all_to_all(copies, axis, split_axis=0, concat_axis=0, tiled=True)  8.99 us
  transfers between devices with their start and end apart: 5, of which 3 were waited for; matrix products, arithmetic and copies ran while one was open for 45% of the time, Pallas kernels for 0%

commit v1 on v0

v1 whole, which is shorter than its diff:
```python
import functools

import jax
import jax.numpy as jnp
from jax import lax
from jax.experimental import pallas as pl
from jax.experimental.pallas import tpu as pltpu
from jax.sharding import Mesh
from jax.sharding import PartitionSpec as P

DH = 128
BLK = 128
PEERS = [(dy, dz) for dy in range(2) for dz in range(8) if (dy, dz) != (0, 0)]
ALL = [(dd, dy, dz) for dd in range(2) for dy in range(2) for dz in range(8) if (dd, dy, dz) != (0, 0, 0)]
MESH = pl.DeviceIdType.MESH
CTX = ("ctx_0", "ctx_1")
F32 = jnp.float32
BF16 = jnp.bfloat16
HIGH = lax.Precision.HIGHEST
LOW = -1e30
SCORE_SCALE = 1.4426950408889634 / (DH**0.5)


def iota(shape, dim):
    return lax.broadcasted_iota(jnp.int32, shape, dim)


def dot(a, b, **kw):
    return jnp.dot(a, b, preferred_element_type=F32, **kw)


def kernel(
    q_ref, k_ref, v_ref, docs_ref, x_ref, gate_ref, b_ref, c_ref, dtr_ref, small_ref, gain_ref,
    teacher_ref, student_ref, ggain_ref, gskip_ref,
    kv, qt, acc, top, total, doc_start, mixed, reach_wide,
    send_s, recv_s, send_e, recv_e, send_g, recv_g,
    ring_send, ring_recv, yf_send, yf_recv, yb_send, yb_recv,
    s_send, s_recv, e_send, e_recv, g_send, g_recv,
):
    dp = lax.axis_index("dp")
    y = lax.axis_index("ctx_0")
    z = lax.axis_index("ctx_1")
    core = lax.rem(lax.axis_index("head"), 2)
    b = y * 8 + z
    me = dp * 16 + b
    way = 1 - 2 * core

    def zmod(v):
        return lax.rem(v + 16, 8)

    def at(dy, dz):
        return {"ctx_0": lax.rem(y + dy, 2), "ctx_1": zmod(z + dz)}

    barrier = pltpu.get_barrier_semaphore()
    for dd, dy, dz in ALL:
        where = {"dp": lax.rem(dp + dd, 2), **at(dy, dz)}
        pl.semaphore_signal(barrier, inc=1, device_id=where, device_id_type=MESH)

    docs = docs_ref[...]
    n0 = jnp.sum(jnp.sum((docs < 1).astype(F32), axis=0, keepdims=True), axis=1, keepdims=True)
    n1 = jnp.sum(jnp.sum((docs < 2).astype(F32), axis=0, keepdims=True), axis=1, keepdims=True)

    expand = (lax.shift_right_logical(iota((16, 1024), 1), 6) == iota((16, 1024), 0)).astype(F32)

    def wide(v):
        return dot(v, expand, precision=HIGH)

    small = small_ref[...]
    dt_bias, decay_log, skip = small[0:1], small[1:2], small[2:3]
    skip_wide = wide(jnp.broadcast_to(skip, (8, 16)))[0:1]
    row_t = iota((BLK, BLK), 0)
    lane_s = iota((BLK, BLK), 1)
    lower = row_t >= lane_s
    lower_f = lower.astype(F32)
    first_lanes = lane_s < 64

    for half in range(2):
        r0 = half * BLK
        block = b if half == 0 else 31 - b
        first = (block * BLK).astype(F32)
        doc_row = docs_ref[pl.ds(block, 1), :]
        start = jnp.where(doc_row == 0, 0.0, jnp.where(doc_row == 1, n0, n1)) - first
        end = jnp.where(doc_row == 0, n0, jnp.where(doc_row == 1, n1, 4096.0)) - first
        doc_start[half] = jnp.broadcast_to(start + first, (8, BLK))
        start_last = start[:, BLK - 1 : BLK]
        inherited = jnp.sum((start < 0.0).astype(F32), axis=1, keepdims=True)

        raw = dtr_ref[0, r0 : r0 + BLK, :] + dt_bias
        dt = jnp.maximum(raw, 0.0) + jnp.log(1.0 + jnp.exp(-jnp.abs(raw)))
        rate = -dt * jnp.exp(decay_log)
        cum = dot(lower_f, rate, precision=HIGH)
        cum_t = cum.T
        dt_t = dt.T
        last = cum[BLK - 1 : BLK, :]
        rows16 = iota((BLK, 16), 0).astype(F32)
        tail = jnp.where(rows16 >= start_last, jnp.exp(last - cum) * dt, 0.0)
        reach = jnp.where(rows16 < inherited, jnp.exp(cum), 0.0)
        decay = jnp.where(start_last < 0.0, jnp.exp(last), 0.0)
        reach_wide[r0 : r0 + BLK, :] = wide(reach)
        tail_wide = wide(tail)
        decay_wide = wide(jnp.broadcast_to(decay, (8, 16)))[0:1]
        if half == 0:
            decay_front = decay_wide
        else:
            decay_back = decay_wide

        bmat = b_ref[0, r0 : r0 + BLK, :]
        cmat = c_ref[0, r0 : r0 + BLK, :]
        xs = x_ref[0, r0 : r0 + BLK, :]
        loaded = (xs.astype(F32) * tail_wide).astype(BF16)
        state = dot(bmat.T, loaded).astype(BF16)
        for j in range(8):
            for n in range(2):
                send_s[n * 8 + j, half * 64 : half * 64 + 64, :] = state[
                    n * 64 : n * 64 + 64, j * BLK : (j + 1) * BLK
                ]
        gram = lax.dot_general(cmat, bmat, (((1,), (1,)), ((), ())), preferred_element_type=F32)
        gram = jnp.where(lower & (row_t.astype(F32) < end), gram, 0.0)
        for j in range(8):
            cols = slice(j * BLK, (j + 1) * BLK)
            pair = x_ref[0, r0 : r0 + BLK, cols]
            parts = []
            for h in (2 * j, 2 * j + 1):
                fading = jnp.exp(cum[:, h : h + 1] - cum_t[h : h + 1, :])
                parts.append((fading * (gram * dt_t[h : h + 1, :])).astype(BF16))
            zero = jnp.zeros_like(pair)
            stacked = jnp.concatenate(
                [jnp.where(first_lanes, pair, zero), jnp.where(first_lanes, zero, pair)], axis=0
            )
            intra = dot(jnp.concatenate(parts, axis=1), stacked)
            mixed[r0 : r0 + BLK, cols] = intra + skip_wide[:, cols] * pair.astype(F32)

    row16 = iota((16, BLK), 0)
    for j in range(8):
        cols = slice(j * BLK, (j + 1) * BLK)
        rows = jnp.zeros((16, BLK), F32)
        for at_row, values in ((0, decay_front), (2, decay_back)):
            value = values[:, cols]
            high = value.astype(BF16).astype(F32)
            rows = jnp.where(row16 == at_row, high, rows)
            rows = jnp.where(row16 == at_row + 1, value - high, rows)
        for n in range(2):
            send_s[n * 8 + j, 128:144, :] = rows.astype(BF16)

    for half in range(2):
        r0 = half * BLK
        kv[b, half, 0] = k_ref[0, r0 : r0 + BLK, :]
        kv[b, half, 1] = v_ref[0, r0 : r0 + BLK, :]

    pl.semaphore_wait(barrier, len(ALL))

    def source(off):
        return zmod(z + off)

    def ring(off, dist, forward):
        sign = way if forward else -way
        s = y * 8 + source(off)
        lane = 0 if forward else 1
        return pltpu.make_async_remote_copy(
            src_ref=kv.at[s], dst_ref=kv.at[s],
            send_sem=ring_send.at[lane, dist], recv_sem=ring_recv.at[s],
            device_id={"ctx_1": zmod(z + sign)}, device_id_type=MESH,
        )

    def y_front(zs, mine):
        s = (y if mine else 1 - y) * 8 + zs
        return pltpu.make_async_remote_copy(
            src_ref=kv.at[s, 0], dst_ref=kv.at[s, 0], send_sem=yf_send.at[zs], recv_sem=yf_recv.at[zs],
            device_id={"ctx_0": 1 - y}, device_id_type=MESH,
        )

    def y_back(zs, mine):
        s = (y if mine else 1 - y) * 8 + zs
        return pltpu.make_async_remote_copy(
            src_ref=kv.at[s, 1], dst_ref=kv.at[s, 1], send_sem=yb_send.at[zs], recv_sem=yb_recv.at[zs],
            device_id={"ctx_0": 1 - y}, device_id_type=MESH,
        )

    def y_start(zs):
        y_front(zs, True).start()

        @pl.when(y == 1)
        def _():
            y_back(zs, True).start()

    def y_arrived(zs):
        y_front(zs, False).wait_recv()

        @pl.when(y == 0)
        def _():
            y_back(zs, False).wait_recv()

    ring(0, 0, True).start()
    ring(0, 0, False).start()
    y_start(z)

    def s_copy(dy, dz):
        other = at(dy, dz)
        o = other["ctx_0"] * 8 + other["ctx_1"]
        return pltpu.make_async_remote_copy(
            src_ref=send_s.at[o], dst_ref=recv_s.at[b], send_sem=s_send.at[o], recv_sem=s_recv.at[b],
            device_id=other, device_id_type=MESH,
        )

    def e_copy(dy, dz):
        other = at(dy, dz)
        o = other["ctx_0"] * 8 + other["ctx_1"]
        return pltpu.make_async_remote_copy(
            src_ref=send_e.at[o], dst_ref=recv_e.at[b], send_sem=e_send.at[o], recv_sem=e_recv.at[b],
            device_id=other, device_id_type=MESH,
        )

    for dy, dz in PEERS:
        s_copy(dy, dz).start()
    recv_s[b] = send_s[b]

    for half in range(2):
        for h in range(8):
            qt[half, :, h * DH : (h + 1) * DH] = q_ref[
                0, half * BLK : (half + 1) * BLK, h * DH : (h + 1) * DH
            ].T
    top[...] = jnp.full(top.shape, LOW, F32)
    total[...] = jnp.zeros(total.shape, F32)
    acc[...] = jnp.zeros(acc.shape, F32)
    row_f = row_t.astype(F32)

    def item(s, kh, qh, diagonal):
        key = kv[s, kh, 0]
        value_t = kv[s, kh, 1].T
        key_block = jnp.where(kh == 0, s, 31 - s) if not isinstance(kh, int) else (s if kh == 0 else 31 - s)
        start = doc_start[qh][0:1] - (key_block * BLK).astype(F32)
        allowed = row_f >= start
        if diagonal:
            allowed = allowed & (row_t <= lane_s)
        bias = jnp.where(allowed, 0.0, LOW)
        bias = jnp.concatenate([bias, bias], axis=1)
        for c in range(4):
            cols = slice(c * 256, (c + 1) * 256)
            scores = dot(key, qt[qh, :, cols]) * SCORE_SCALE + bias
            old = top[qh, :, cols]
            new = jnp.maximum(old, jnp.max(scores, axis=0, keepdims=True))
            weights = jnp.exp2(scores - new)
            factor = jnp.exp2(old - new)
            total[qh, :, cols] = total[qh, :, cols] * factor + jnp.sum(weights, axis=0, keepdims=True)
            acc[qh, :, cols] = acc[qh, :, cols] * factor + dot(value_t, weights.astype(BF16))
            top[qh, :, cols] = new

    def other_source(s):
        earlier = s < b
        item(s, 0, 1, False)
        pick = jnp.where(earlier, 0, 1)
        item(s, pick, pick, False)

    def sources(ids):
        def step(i, carry):
            s = ids[0]
            for n in range(1, len(ids)):
                s = jnp.where(i == n, ids[n], s)
            other_source(s)
            return carry

        lax.fori_loop(0, len(ids), step, 0)

    item(b, 0, 0, True)
    item(b, 1, 1, True)
    item(b, 0, 1, False)

    def mine(zs):
        return y * 8 + zs

    def theirs(zs):
        return (1 - y) * 8 + zs

    def hop(d):
        ids = []
        up = source(-way * d)
        ring(-way * d, 0, True).wait_recv()
        if d < 4:
            ring(-way * d, d, True).start()
        y_start(up)
        ids.append(mine(up))
        if d < 4:
            down = source(way * d)
            ring(way * d, 0, False).wait_recv()
            if d < 3:
                ring(way * d, d, False).start()
            y_start(down)
            ids.append(mine(down))
        if d == 1:
            y_arrived(z)
            ids.append(theirs(z))
        else:
            for off in (-way * (d - 1), way * (d - 1)):
                y_arrived(source(off))
                ids.append(theirs(source(off)))
        sources(ids)

    hop(1)
    hop(2)

    def s_wait(k):
        @pl.when(k != b)
        def _():
            pltpu.make_async_remote_copy(
                src_ref=send_s.at[k], dst_ref=recv_s.at[k], send_sem=s_send.at[k], recv_sem=s_recv.at[k],
                device_id={"ctx_1": z}, device_id_type=MESH,
            ).wait_recv()

    def forward(k, state):
        s_wait(k)
        send_e[k, 0:64, :] = state.astype(BF16)
        rows = recv_s[k, 128:144, :].astype(F32)
        return (rows[0:1] + rows[1:2]) * state + recv_s[k, 0:64, :].astype(F32)

    def backward(i, state):
        k = 15 - i
        send_e[k, 64:128, :] = state.astype(BF16)
        rows = recv_s[k, 128:144, :].astype(F32)
        return (rows[2:3] + rows[3:4]) * state + recv_s[k, 64:128, :].astype(F32)

    state = lax.fori_loop(0, 16, forward, jnp.zeros((64, BLK), F32))
    lax.fori_loop(0, 16, backward, state)
    for dy, dz in PEERS:
        e_copy(dy, dz).start()
    recv_e[b] = send_e[b]

    hop(3)
    hop(4)
    y_arrived(source(-way * 4))
    other_source(theirs(source(-way * 4)))

    for half in range(2):
        for h in range(8):
            cols = slice(h * DH, (h + 1) * DH)
            out = acc[half, :, cols] / total[half, :, cols]
            teacher_ref[0, half * BLK : (half + 1) * BLK, cols] = out.T.astype(BF16)

    for dy, dz in PEERS:
        other = at(dy, dz)
        o = other["ctx_0"] * 8 + other["ctx_1"]
        pltpu.make_async_remote_copy(
            src_ref=send_e.at[o], dst_ref=recv_e.at[o], send_sem=e_send.at[o], recv_sem=e_recv.at[o],
            device_id=other, device_id_type=MESH,
        ).wait_recv()
    for half in range(2):
        r0 = half * BLK
        cmat = c_ref[0, r0 : r0 + BLK, :]
        for j in range(8):
            cols = slice(j * BLK, (j + 1) * BLK)
            part = slice(half * 64, half * 64 + 64)
            entering = jnp.concatenate([recv_e[j, part, :], recv_e[8 + j, part, :]], axis=0)
            flow = dot(cmat, entering)
            mixed[r0 : r0 + BLK, cols] = mixed[r0 : r0 + BLK, cols] + flow * reach_wide[r0 : r0 + BLK, cols]

    gain = gain_ref[...]
    rows_at_once = 16

    def norm(i, carry):
        by_gain, by_skip = carry
        rows = pl.ds(pl.multiple_of(i * rows_at_once, rows_at_once), rows_at_once)
        gate = gate_ref[0, rows, :].astype(F32)
        silu = gate / (1.0 + jnp.exp(-gate))
        gated = mixed[rows, :] * silu
        mean = jnp.sum(gated * gated, axis=1, keepdims=True) * (1.0 / 1024)
        inv = lax.rsqrt(mean + 1e-05)
        unit = gated * inv
        normed = unit * gain
        student_ref[0, rows, :] = normed.astype(BF16)
        grad = (normed - teacher_ref[0, rows, :].astype(F32)) * (2.0 / 8192)
        g_unit = grad * gain
        along = jnp.sum(g_unit * unit, axis=1, keepdims=True) * (1.0 / 1024)
        g_mixed = (g_unit - unit * along) * inv * silu
        a = grad * unit
        c = g_mixed * x_ref[0, rows, :].astype(F32)
        return by_gain + a[0:8] + a[8:16], by_skip + c[0:8] + c[8:16]

    zero = jnp.zeros((8, 1024), F32)
    by_gain, by_skip = lax.fori_loop(0, 256 // rows_at_once, norm, (zero, zero))
    by_gain = jnp.sum(by_gain, axis=0, keepdims=True)
    by_head = lax.dot_general(
        by_skip, expand, (((1,), (1,)), ((), ())), preferred_element_type=F32, precision=HIGH
    )
    by_head = jnp.sum(by_head, axis=0, keepdims=True)
    for r in range(8):
        send_g[r : r + 1, :] = by_gain[:, r * BLK : (r + 1) * BLK]
    send_g[8:16, :] = jnp.zeros((8, BLK), F32)
    send_g[8:9, 0:16] = by_head

    def g_copy(dd, dy, dz, arriving):
        where = {"dp": lax.rem(dp + dd, 2), **at(dy, dz)}
        o = where["dp"] * 16 + where["ctx_0"] * 8 + where["ctx_1"]
        slot = o if arriving else me
        return pltpu.make_async_remote_copy(
            src_ref=send_g, dst_ref=recv_g.at[slot], send_sem=g_send.at[o], recv_sem=g_recv.at[slot],
            device_id=where, device_id_type=MESH,
        )

    for peer in ALL:
        g_copy(*peer, False).start()
    recv_g[me] = send_g[...]
    for peer in ALL:
        g_copy(*peer, True).wait_recv()
    summed = recv_g[0]
    for n in range(1, 32):
        summed = summed + recv_g[n]
    ggain_ref[...] = summed[0:8]
    gskip_ref[...] = summed[8:9, 0:16]

    for d in range(4):
        ring(0, d, True).wait_send()
    for d in range(3):
        ring(0, d, False).wait_send()
    for zs in range(8):
        y_front(zs, True).wait_send()

        @pl.when(y == 1)
        def _():
            y_back(zs, True).wait_send()

    for dy, dz in PEERS:
        s_copy(dy, dz).wait_send()
        e_copy(dy, dz).wait_send()
    for peer in ALL:
        g_copy(*peer, False).wait_send()


def body(
    queries, keys, values, doc_ids, inputs, gate_input, b_input, c_input, dt_raw, dt_bias, decay_log, skip, gain
):
    small = jnp.stack([dt_bias, decay_log, skip])
    vmem = pl.BlockSpec(memory_space=pltpu.VMEM)
    dma = pltpu.SemaphoreType.DMA
    teacher, student, by_gain, by_skip = pl.pallas_call(
        kernel,
        out_shape=(
            jax.ShapeDtypeStruct((1, 256, 1024), BF16),
            jax.ShapeDtypeStruct((1, 256, 1024), BF16),
            jax.ShapeDtypeStruct((8, 128), F32),
            jax.ShapeDtypeStruct((1, 16), F32),
        ),
        in_specs=[vmem] * 11,
        out_specs=(vmem,) * 4,
        scratch_shapes=[
            pltpu.VMEM((16, 2, 2, BLK, DH), BF16),
            pltpu.VMEM((2, DH, 1024), BF16),
            pltpu.VMEM((2, DH, 1024), F32),
            pltpu.VMEM((2, 1, 1024), F32),
            pltpu.VMEM((2, 1, 1024), F32),
            pltpu.VMEM((2, 8, BLK), F32),
            pltpu.VMEM((256, 1024), F32),
            pltpu.VMEM((256, 1024), F32),
            pltpu.VMEM((16, 144, BLK), BF16),
            pltpu.VMEM((16, 144, BLK), BF16),
            pltpu.VMEM((16, BLK, BLK), BF16),
            pltpu.VMEM((16, BLK, BLK), BF16),
            pltpu.VMEM((16, BLK), F32),
            pltpu.VMEM((32, 16, BLK), F32),
            dma((2, 4)), dma((16,)), dma((8,)), dma((8,)), dma((8,)), dma((8,)),
            dma((16,)), dma((16,)), dma((16,)), dma((16,)), dma((32,)), dma((32,)),
        ],
        compiler_params=pltpu.CompilerParams(
            collective_id=0, has_side_effects=True, vmem_limit_bytes=48 * 1024 * 1024
        ),
    )(
        queries, keys, values, doc_ids.reshape(32, 128), inputs, gate_input, b_input, c_input, dt_raw,
        small, gain.reshape(1, 1024),
    )
    return teacher, student, by_gain.reshape(1024), by_skip.reshape(16)


def solution(mesh):
    split = Mesh(
        mesh.devices.reshape(mesh.shape["dp"], 2, 8, mesh.shape["head"]),
        ("dp", "ctx_0", "ctx_1", "head"),
    )
    rows = P("dp", CTX, "head")
    return jax.shard_map(
        body,
        mesh=split,
        in_specs=(rows, rows, rows, P("dp", None), rows, rows, rows, rows, rows)
        + (P("head"),) * 4,
        out_specs=(rows, rows, P("head"), P("head")),
        check_vma=False,
    )
```

time: 261 us -> 76.8 us (0.29)
  Pallas kernels: 0 us -> 66.1 us
  blocking collectives: 65.9 us -> 0 us
  local copies, waits for them, and re-layouts: 54 us -> 9.03 us
  matrix products: 43.1 us -> 0 us
  other arithmetic: 41.6 us -> 0.01 us
  waiting for transfers between devices: 26.7 us -> 0 us
  between operations: 17.5 us -> 0.74 us
  starting transfers between devices: 9.11 us -> 0 us
    pallas_call x0 -> x1, Pallas kernels: none -> 66.1 us  [body(): pl.pallas_call(kernel, out_shape=(jax.ShapeDtypeStruct((1, 256, 1024), BF...]
    all_gather x6 -> x0, blocking collectives: 65.9 us -> none  [the longest x3 38.2 us: entering(): lax.all_gather(part.astype(kind), axis)]
    dot_general x24 -> x0, matrix products: 43.1 us -> none  [the longest x8 16.3 us: inner(): jnp.einsum('tkgs,skd->tkgd', weights.astype(jnp.bfloat16), value_now, pre...]
    gather x3 -> x0, local copies, waits for them, and re-layouts: 25.6 us -> none  [the longest x2 23.6 us: body(): key_docs = jnp.take(docs, key_pos).reshape(size // span, span)]
    all_to_all x2 -> x0, waiting for transfers between devices: 14.1 us -> none  [sent_to_all(): return lax.all_to_all(copies, axis, split_axis=0, concat_axis=0, tiled=True)]
    all_gather x3 -> x0, waiting for transfers between devices: 12.6 us -> none  [the longest x1 12.5 us: sent_together(): result, at, done = (lax.all_gather(both, axis, axis=dim, tiled=True), 0, [])]
    reduce_sum x15 -> x0, other arithmetic: 12.4 us -> none  [the longest x8 6.91 us: inner(): total = total * factor + jnp.sum(weights, axis=3)]
    convert_element_type x10 -> x0, other arithmetic: 10.5 us -> none  [the longest x1 2.11 us: entering(): part.astype(kind)]
  transfers between devices with their start and end apart: 5 -> 0, of which waited for: 3 -> 0; matrix products, arithmetic and copies ran while one was open for 45% -> 0% of each run, Pallas kernels for 0% -> 0%
where the time goes in v1:
time: 76.8 us; the launch traced here: 75.9 us
  Pallas kernels  66.1 us (86%)
  local copies, waits for them, and re-layouts  9.03 us (12%)
    pallas_call x1, Pallas kernels, body(): pl.pallas_call(kernel, out_shape=(jax.ShapeDtypeStruct((1, 256, 1024), BF...  66.1 us
    unnamed x29, local copies, waits for them, and re-layouts  9.03 us

profile of v1, /device:TPU:4, one launch (start us, length us, event | category | flops | bytes accessed | tf_op | source)
XLA Modules:
  0.0 75.9 jit_solution(7626174981937378170)
XLA Ops:
  0.6 0.0 copy-start.9
  0.6 0.0 copy-start.10
  0.7 0.0 copy-start.11
  0.7 0.0 copy-start.8
  0.7 0.6 copy-done.9
  1.3 0.0 copy-done.10
  1.3 0.0 copy-done.11
  1.3 0.0 copy-start.3
  1.3 0.0 copy-start.4
  1.4 0.0 copy-start.7
  1.4 0.9 %copy.17.dtr_ref = f32[1,256,16]{2,1,0:T(8,128)S(1)} copy(f32[1,256,16]{1,2,0:T(8,128)} %param.21) | data formatting | bytes 32768 | tf_op args[8]
  2.2 0.0 copy-done.8
  2.2 0.0 copy-done.3
  2.2 0.0 copy-done.4
  2.3 0.0 copy-done.7
  2.3 0.0 copy-start
  2.3 1.0 %copy-done = bf16[1,256,1024]{2,1,0:T(8,128)(2,1)S(1)} copy-done((bf16[1,256,1024]{2,1,0:T(8,128)(2,1)S(1)}, bf16[1,256,1024]{2,1,0:T(8,128)(2,1)}, u32[]{:S(2)}) %copy-start) | copy-done | bytes 524312
  3.3 0.0 copy-start.1
  3.3 1.0 %copy-done.1 = bf16[1,256,1024]{2,1,0:T(8,128)(2,1)S(1)} copy-done((bf16[1,256,1024]{2,1,0:T(8,128)(2,1)S(1)}, bf16[1,256,1024]{2,1,0:T(8,128)(2,1)}, u32[]{:S(2)}) %copy-start.1) | copy-done | bytes 524312
  4.4 0.0 copy-start.2
  4.4 1.0 %copy-done.2 = bf16[1,256,1024]{2,1,0:T(8,128)(2,1)S(1)} copy-done((bf16[1,256,1024]{2,1,0:T(8,128)(2,1)S(1)}, bf16[1,256,1024]{2,1,0:T(8,128)(2,1)}, u32[]{:S(2)}) %copy-start.2) | copy-done | bytes 524312
  5.4 0.0 copy-start.5
  5.4 0.8 %copy-done.5 = bf16[1,256,128]{2,1,0:T(8,128)(2,1)S(1)} copy-done((bf16[1,256,128]{2,1,0:T(8,128)(2,1)S(1)}, bf16[1,256,128]{2,1,0:T(8,128)(2,1)}, u32[]{:S(2)}) %copy-start.5) | copy-done | bytes 65560
  6.2 0.0 copy-start.6
  6.2 0.8 %copy-done.6 = bf16[1,256,128]{2,1,0:T(8,128)(2,1)S(1)} copy-done((bf16[1,256,128]{2,1,0:T(8,128)(2,1)S(1)}, bf16[1,256,128]{2,1,0:T(8,128)(2,1)}, u32[]{:S(2)}) %copy-start.6) | copy-done | bytes 65560
  7.1 66.1 %shard_map.156 = (bf16[1,256,1024]{2,1,0:T(8,128)(2,1)S(1)}, bf16[1,256,1024]{2,1,0:T(8,128)(2,1)S(1)}, f32[8,128]{1,0:T(8,128)S(1)}, f32[1,16]{1,0:T(1,128)S(1)}) custom-call(bf16[1,256,1024]{2,1,0:T(8,128)(2,1)S(1)} %copy-done, bf16[1,256,128]{2,1,0:T(8,128)(2,1)S(1)} %copy-done.3, bf16[1,256,128]{2,1,0:T(8,128)(2,1)S(1)} %copy-done.4, ...), custom_call_target="tpu_custom_call" | custom-call | tf_op jit(solution)/shard_map/pallas_call | solution.py:433
  73.2 0.8 %copy.22 = bf16[1,256,1024]{2,1,0:T(8,128)(2,1)} copy(bf16[1,256,1024]{2,1,0:T(8,128)(2,1)S(1)} %get-tuple-element.16) | data formatting | bytes 1048576
  74.0 0.8 %copy.23 = bf16[1,256,1024]{2,1,0:T(8,128)(2,1)} copy(bf16[1,256,1024]{2,1,0:T(8,128)(2,1)S(1)} %get-tuple-element.17) | data formatting | bytes 1048576
  74.8 0.6 copy.24
  75.4 0.5 copy.25
  (1 shorter events, 0.0 us)
Async XLA Ops:
  0.6 0.7 copy-start.9
  0.6 0.7 copy-start.10
  0.7 0.7 copy-start.11
  0.7 1.6 %copy-start.8 = (f32[1024]{0:T(1024)S(1)}, f32[1024]{0:T(1024)}, u32[]{:S(2)}) copy-start(f32[1024]{0:T(1024)} %param.25) | copy-start | bytes 12292
  1.3 0.9 %copy-start.3 = (bf16[1,256,128]{2,1,0:T(8,128)(2,1)S(1)}, bf16[1,256,128]{2,1,0:T(8,128)(2,1)}, u32[]{:S(2)}) copy-start(bf16[1,256,128]{2,1,0:T(8,128)(2,1)} %k_ref.1) | copy-start | bytes 196612
  1.3 0.9 %copy-start.4 = (bf16[1,256,128]{2,1,0:T(8,128)(2,1)S(1)}, bf16[1,256,128]{2,1,0:T(8,128)(2,1)}, u32[]{:S(2)}) copy-start(bf16[1,256,128]{2,1,0:T(8,128)(2,1)} %v_ref.1) | copy-start | bytes 196612
  1.4 0.9 %copy-start.7 = (s32[1,4096]{1,0:T(1,128)S(1)}, s32[1,4096]{1,0:T(1,128)}, u32[]{:S(2)}) copy-start(s32[1,4096]{1,0:T(1,128)} %param.16) | copy-start | bytes 49156
  2.3 1.0 %copy-start = (bf16[1,256,1024]{2,1,0:T(8,128)(2,1)S(1)}, bf16[1,256,1024]{2,1,0:T(8,128)(2,1)}, u32[]{:S(2)}) copy-start(bf16[1,256,1024]{2,1,0:T(8,128)(2,1)} %q_ref.1) | copy-start | bytes 1572868
  3.3 1.0 %copy-start.1 = (bf16[1,256,1024]{2,1,0:T(8,128)(2,1)S(1)}, bf16[1,256,1024]{2,1,0:T(8,128)(2,1)}, u32[]{:S(2)}) copy-start(bf16[1,256,1024]{2,1,0:T(8,128)(2,1)} %x_ref.1) | copy-start | bytes 1572868
  4.4 1.0 %copy-start.2 = (bf16[1,256,1024]{2,1,0:T(8,128)(2,1)S(1)}, bf16[1,256,1024]{2,1,0:T(8,128)(2,1)}, u32[]{:S(2)}) copy-start(bf16[1,256,1024]{2,1,0:T(8,128)(2,1)} %gate_ref.1) | copy-start | bytes 1572868
  5.4 0.8 %copy-start.5 = (bf16[1,256,128]{2,1,0:T(8,128)(2,1)S(1)}, bf16[1,256,128]{2,1,0:T(8,128)(2,1)}, u32[]{:S(2)}) copy-start(bf16[1,256,128]{2,1,0:T(8,128)(2,1)} %b_ref.1) | copy-start | bytes 196612
  6.2 0.8 %copy-start.6 = (bf16[1,256,128]{2,1,0:T(8,128)(2,1)S(1)}, bf16[1,256,128]{2,1,0:T(8,128)(2,1)}, u32[]{:S(2)}) copy-start(bf16[1,256,128]{2,1,0:T(8,128)(2,1)} %c_ref.1) | copy-start | bytes 196612

commit v2 on v1

v2 whole, which is shorter than its diff:
```python
import functools

import jax
import jax.numpy as jnp
from jax import lax
from jax.experimental import pallas as pl
from jax.experimental.pallas import tpu as pltpu
from jax.sharding import Mesh
from jax.sharding import PartitionSpec as P

DH = 128
BLK = 128
PEERS = [(dy, dz) for dy in range(2) for dz in range(8) if (dy, dz) != (0, 0)]
ALL = [(dd, dy, dz) for dd in range(2) for dy in range(2) for dz in range(8) if (dd, dy, dz) != (0, 0, 0)]
MESH = pl.DeviceIdType.MESH
CTX = ("ctx_0", "ctx_1")
F32 = jnp.float32
BF16 = jnp.bfloat16
HIGH = lax.Precision.HIGHEST
LOW = -1e30
SCORE_SCALE = 1.4426950408889634 / (DH**0.5)


def iota(shape, dim):
    return lax.broadcasted_iota(jnp.int32, shape, dim)


def dot(a, b, **kw):
    return jnp.dot(a, b, preferred_element_type=F32, **kw)


def kernel(
    q_hbm, k_hbm, v_hbm, docs_hbm, x_hbm, gate_hbm, b_hbm, c_hbm, dtr_hbm, bias_hbm, decay_hbm, skip_hbm, gain_hbm,
    teacher_hbm, student_hbm, ggain_ref, gskip_ref,
    teacher_ref, student_ref, q_ref, docs_ref, x_ref, gate_ref, b_ref, c_ref, dtr_ref, bias_ref, decay_ref, skip_ref, gain_ref,
    kv, qt, acc, top, total, doc_start, mixed, reach_wide,
    send_s, recv_s, send_d, recv_d, send_e, recv_e, send_g, recv_g,
    in_sem, out_sem, kv_sem, ring_send, ring_recv, y_send, y_recv,
    s_send, s_recv, d_send, d_recv, e_send, e_recv, g_send, g_recv,
):
    dp = lax.axis_index("dp")
    y = lax.axis_index("ctx_0")
    z = lax.axis_index("ctx_1")
    core = lax.rem(lax.axis_index("head"), 2)
    b = y * 8 + z
    me = dp * 16 + b
    way = 1 - 2 * core

    def zmod(v):
        return lax.rem(v + 16, 8)

    def at(dy, dz):
        return {"ctx_0": lax.rem(y + dy, 2), "ctx_1": zmod(z + dz)}

    barrier = pltpu.get_barrier_semaphore()
    for dd, dy, dz in ALL:
        where = {"dp": lax.rem(dp + dd, 2), **at(dy, dz)}
        pl.semaphore_signal(barrier, inc=1, device_id=where, device_id_type=MESH)

    arrays = (
        (docs_hbm, docs_ref), (dtr_hbm, dtr_ref), (bias_hbm, bias_ref), (decay_hbm, decay_ref),
        (skip_hbm, skip_ref), (x_hbm, x_ref), (b_hbm, b_ref), (c_hbm, c_ref),
        (q_hbm, q_ref), (gate_hbm, gate_ref), (gain_hbm, gain_ref),
    )
    loads = [pltpu.make_async_copy(src, dst, in_sem.at[n]) for n, (src, dst) in enumerate(arrays)]
    for load in loads[:8]:
        load.start()
    kv_loads = []
    for half in range(2):
        for n, src in enumerate((k_hbm, v_hbm)):
            kv_loads.append(
                pltpu.make_async_copy(
                    src.at[0, half * BLK : (half + 1) * BLK, :], kv.at[b, half, n], kv_sem.at[half, n]
                )
            )
    for load in kv_loads:
        load.start()
    for load in loads[8:]:
        load.start()
    for load in loads[:8]:
        load.wait()

    docs = docs_ref[...]
    n0 = jnp.sum(jnp.sum((docs < 1).astype(F32), axis=0, keepdims=True), axis=1, keepdims=True)
    n1 = jnp.sum(jnp.sum((docs < 2).astype(F32), axis=0, keepdims=True), axis=1, keepdims=True)

    expand = (lax.shift_right_logical(iota((16, 1024), 1), 6) == iota((16, 1024), 0)).astype(F32)

    def wide(v):
        return dot(v, expand, precision=HIGH)

    skip_wide = wide(jnp.broadcast_to(skip_ref[...], (8, 16)))[0:1]
    row_t = iota((BLK, BLK), 0)
    lane_s = iota((BLK, BLK), 1)
    row_f = row_t.astype(F32)
    lower = row_t >= lane_s
    lower_f = lower.astype(F32)
    first_lanes = lane_s < 64

    def local_terms(half):
        r0 = half * BLK
        block = b if half == 0 else 31 - b
        first = (block * BLK).astype(F32)
        doc_row = docs_ref[pl.ds(block, 1), :]
        start = jnp.where(doc_row == 0, 0.0, jnp.where(doc_row == 1, n0, n1)) - first
        end = jnp.where(doc_row == 0, n0, jnp.where(doc_row == 1, n1, 4096.0)) - first
        doc_start[half] = jnp.broadcast_to(start + first, (8, BLK))
        start_last = start[:, BLK - 1 : BLK]
        inherited = jnp.sum((start < 0.0).astype(F32), axis=1, keepdims=True)

        raw = dtr_ref[0, :, r0 : r0 + BLK].T + bias_ref[...]
        dt = jnp.maximum(raw, 0.0) + jnp.log(1.0 + jnp.exp(-jnp.abs(raw)))
        rate = -dt * jnp.exp(decay_ref[...])
        cum = dot(lower_f, rate, precision=HIGH)
        cum_t = cum.T
        dt_t = dt.T
        last = cum[BLK - 1 : BLK, :]
        rows16 = iota((BLK, 16), 0).astype(F32)
        tail = jnp.where(rows16 >= start_last, jnp.exp(last - cum) * dt, 0.0)
        reach = jnp.where(rows16 < inherited, jnp.exp(cum), 0.0)
        decay = jnp.where(start_last < 0.0, jnp.exp(last), 0.0)
        tail_wide = wide(tail)
        decay_wide = wide(jnp.broadcast_to(decay, (8, 16)))[0:1]

        bmat = b_ref[0, r0 : r0 + BLK, :]
        cmat = c_ref[0, r0 : r0 + BLK, :]
        loaded = (x_ref[0, r0 : r0 + BLK, :].astype(F32) * tail_wide).astype(BF16)
        state = dot(bmat.T, loaded).astype(BF16)
        for j in range(8):
            cols = slice(j * BLK, (j + 1) * BLK)
            send_d[j, half : half + 1, :] = decay_wide[:, cols]
            for n in range(2):
                send_s[n * 8 + j, half] = state[n * 64 : n * 64 + 64, cols]

        def rest():
            reach_wide[r0 : r0 + BLK, :] = wide(reach)
            gram = lax.dot_general(cmat, bmat, (((1,), (1,)), ((), ())), preferred_element_type=F32)
            gram = jnp.where(lower & (row_f < end), gram, 0.0)
            for j in range(8):
                cols = slice(j * BLK, (j + 1) * BLK)
                pair = x_ref[0, r0 : r0 + BLK, cols]
                parts = []
                for h in (2 * j, 2 * j + 1):
                    fading = jnp.exp(cum[:, h : h + 1] - cum_t[h : h + 1, :])
                    parts.append((fading * (gram * dt_t[h : h + 1, :])).astype(BF16))
                zero = jnp.zeros_like(pair)
                stacked = jnp.concatenate(
                    [jnp.where(first_lanes, pair, zero), jnp.where(first_lanes, zero, pair)], axis=0
                )
                intra = dot(jnp.concatenate(parts, axis=1), stacked)
                mixed[r0 : r0 + BLK, cols] = intra + skip_wide[:, cols] * pair.astype(F32)

        return rest

    def source(off):
        return zmod(z + off)

    def ring(off, dist, forward, half):
        s = y * 8 + source(off)
        lane = 0 if forward else 1
        return pltpu.make_async_remote_copy(
            src_ref=kv.at[s, half], dst_ref=kv.at[s, half],
            send_sem=ring_send.at[lane, dist, half], recv_sem=ring_recv.at[s, half],
            device_id={"ctx_1": zmod(z + (way if forward else -way))}, device_id_type=MESH,
        )

    def y_copy(zs, half, mine):
        s = (y if mine else 1 - y) * 8 + zs
        return pltpu.make_async_remote_copy(
            src_ref=kv.at[s, half], dst_ref=kv.at[s, half],
            send_sem=y_send.at[zs, half], recv_sem=y_recv.at[zs, half],
            device_id={"ctx_0": 1 - y}, device_id_type=MESH,
        )

    def y_start(zs, half):
        if half == 0:
            y_copy(zs, 0, True).start()
        else:

            @pl.when(y == 1)
            def _():
                y_copy(zs, 1, True).start()

    def y_arrived(zs):
        y_copy(zs, 0, False).wait_recv()

        @pl.when(y == 0)
        def _():
            y_copy(zs, 1, False).wait_recv()

    def owner(dy, dz):
        other = at(dy, dz)
        return other, other["ctx_0"] * 8 + other["ctx_1"]

    def s_copy(dy, dz, half):
        other, o = owner(dy, dz)
        return pltpu.make_async_remote_copy(
            src_ref=send_s.at[o, half], dst_ref=recv_s.at[b, half],
            send_sem=s_send.at[o, half], recv_sem=s_recv.at[b, half],
            device_id=other, device_id_type=MESH,
        )

    def d_copy(dy, dz):
        other, o = owner(dy, dz)
        return pltpu.make_async_remote_copy(
            src_ref=send_d.at[other["ctx_1"]], dst_ref=recv_d.at[b], send_sem=d_send.at[o], recv_sem=d_recv.at[b],
            device_id=other, device_id_type=MESH,
        )

    def e_copy(dy, dz, half, arriving=False):
        other, o = owner(dy, dz)
        slot = o if arriving else b
        return pltpu.make_async_remote_copy(
            src_ref=send_e.at[o, half], dst_ref=recv_e.at[slot, half],
            send_sem=e_send.at[o, half], recv_sem=e_recv.at[slot, half],
            device_id=other, device_id_type=MESH,
        )

    rest = local_terms(0)
    for load in kv_loads:
        load.wait()
    pl.semaphore_wait(barrier, len(ALL))

    for half in range(2):
        ring(0, 0, True, half).start()
        ring(0, 0, False, half).start()
        y_start(z, half)
    for dy, dz in PEERS:
        s_copy(dy, dz, 0).start()
    rest()
    rest = local_terms(1)
    recv_s[b] = send_s[b]
    recv_d[b] = send_d[z]

    loads[8].wait()
    for half in range(2):
        for h in range(8):
            qt[half, :, h * DH : (h + 1) * DH] = q_ref[
                0, half * BLK : (half + 1) * BLK, h * DH : (h + 1) * DH
            ].T
    top[...] = jnp.full(top.shape, LOW, F32)
    total[...] = jnp.zeros(total.shape, F32)
    acc[...] = jnp.zeros(acc.shape, F32)

    def item(s, kh, qh, diagonal):
        key = kv[s, kh, 0]
        value_t = kv[s, kh, 1].T
        key_block = jnp.where(kh == 0, s, 31 - s) if not isinstance(kh, int) else (s if kh == 0 else 31 - s)
        start = doc_start[qh][0:1] - (key_block * BLK).astype(F32)
        allowed = row_f >= start
        if diagonal:
            allowed = allowed & (row_t <= lane_s)
        bias = jnp.where(allowed, 0.0, LOW)
        bias = jnp.concatenate([bias, bias], axis=1)
        for c in range(4):
            cols = slice(c * 256, (c + 1) * 256)
            scores = dot(key, qt[qh, :, cols]) * SCORE_SCALE + bias
            old = top[qh, :, cols]
            new = jnp.maximum(old, jnp.max(scores, axis=0, keepdims=True))
            weights = jnp.exp2(scores - new)
            factor = jnp.exp2(old - new)
            total[qh, :, cols] = total[qh, :, cols] * factor + jnp.sum(weights, axis=0, keepdims=True)
            acc[qh, :, cols] = acc[qh, :, cols] * factor + dot(value_t, weights.astype(BF16))
            top[qh, :, cols] = new

    def other_source(s):
        item(s, 0, 1, False)
        pick = jnp.where(s < b, 0, 1)
        item(s, pick, pick, False)

    def sources(ids):
        def step(i, carry):
            s = ids[0]
            for n in range(1, len(ids)):
                s = jnp.where(i == n, ids[n], s)
            other_source(s)
            return carry

        lax.fori_loop(0, len(ids), step, 0)

    def mine(zs):
        return y * 8 + zs

    def theirs(zs):
        return (1 - y) * 8 + zs

    def hop(d):
        up = source(-way * d)
        down = source(way * d)
        for half in range(2):
            ring(-way * d, 0, True, half).wait_recv()
            if d < 4:
                ring(-way * d, d, True, half).start()
            y_start(up, half)
            if d < 4:
                ring(way * d, 0, False, half).wait_recv()
                if d < 3:
                    ring(way * d, d, False, half).start()
                y_start(down, half)

    def attend(d):
        ids = [mine(source(-way * d))]
        if d < 4:
            ids.append(mine(source(way * d)))
        if d == 1:
            y_arrived(z)
            ids.append(theirs(z))
        else:
            for off in (-way * (d - 1), way * (d - 1)):
                y_arrived(source(off))
                ids.append(theirs(source(off)))
        sources(ids)

    hop(1)
    for dy, dz in PEERS:
        d_copy(dy, dz).start()
        s_copy(dy, dz, 1).start()
    rest()
    item(b, 0, 0, True)
    item(b, 1, 1, True)
    item(b, 0, 1, False)
    attend(1)
    hop(2)

    def s_wait(k, half):
        @pl.when(k != b)
        def _():
            pltpu.make_async_remote_copy(
                src_ref=send_s.at[k, half], dst_ref=recv_s.at[k, half],
                send_sem=s_send.at[k, half], recv_sem=s_recv.at[k, half],
                device_id={"ctx_1": z}, device_id_type=MESH,
            ).wait_recv()
            if half == 0:
                pltpu.make_async_remote_copy(
                    src_ref=send_d.at[0], dst_ref=recv_d.at[k], send_sem=d_send.at[k], recv_sem=d_recv.at[k],
                    device_id={"ctx_1": z}, device_id_type=MESH,
                ).wait_recv()

    def scan(half, state):
        def step(i, state):
            k = i if half == 0 else 15 - i
            s_wait(k, half)
            send_e[k, half] = state.astype(BF16)
            return recv_d[k, half : half + 1, :] * state + recv_s[k, half].astype(F32)

        state = lax.fori_loop(0, 16, step, state)
        for dy, dz in PEERS:
            e_copy(dy, dz, half).start()
        recv_e[b, half] = send_e[b, half]
        return state

    state = scan(0, jnp.zeros((64, BLK), F32))
    attend(2)
    hop(3)
    scan(1, state)
    attend(3)
    hop(4)
    attend(4)
    y_arrived(source(-way * 4))
    other_source(theirs(source(-way * 4)))

    for load in loads[9:]:
        load.wait()
    gain = gain_ref[...]
    rows_at_once = 16

    def norm(i, carry):
        by_gain, by_skip = carry
        rows = pl.ds(pl.multiple_of(i * rows_at_once, rows_at_once), rows_at_once)
        gate = gate_ref[0, rows, :].astype(F32)
        silu = gate / (1.0 + jnp.exp(-gate))
        gated = mixed[rows, :] * silu
        mean = jnp.sum(gated * gated, axis=1, keepdims=True) * (1.0 / 1024)
        inv = lax.rsqrt(mean + 1e-05)
        unit = gated * inv
        normed = unit * gain
        student_ref[0, rows, :] = normed.astype(BF16)
        grad = (normed - teacher_ref[0, rows, :].astype(F32)) * (2.0 / 8192)
        g_unit = grad * gain
        along = jnp.sum(g_unit * unit, axis=1, keepdims=True) * (1.0 / 1024)
        g_mixed = (g_unit - unit * along) * inv * silu
        a = grad * unit
        c = g_mixed * x_ref[0, rows, :].astype(F32)
        return by_gain + a[0:8] + a[8:16], by_skip + c[0:8] + c[8:16]

    zero = jnp.zeros((8, 1024), F32)
    grads = (zero, zero)
    for half in range(2):
        r0 = half * BLK
        for h in range(8):
            cols = slice(h * DH, (h + 1) * DH)
            out = acc[half, :, cols] / total[half, :, cols]
            teacher_ref[0, r0 : r0 + BLK, cols] = out.T.astype(BF16)
    outputs = (
        pltpu.make_async_copy(teacher_ref, teacher_hbm, out_sem.at[0]),
        pltpu.make_async_copy(student_ref, student_hbm, out_sem.at[1]),
    )
    outputs[0].start()
    for half in range(2):
        r0 = half * BLK
        for dy, dz in PEERS:
            e_copy(dy, dz, half, True).wait_recv()
        cmat = c_ref[0, r0 : r0 + BLK, :]
        for j in range(8):
            cols = slice(j * BLK, (j + 1) * BLK)
            flow = dot(cmat, jnp.concatenate([recv_e[j, half], recv_e[8 + j, half]], axis=0))
            mixed[r0 : r0 + BLK, cols] = mixed[r0 : r0 + BLK, cols] + flow * reach_wide[r0 : r0 + BLK, cols]
        steps = BLK // rows_at_once
        grads = lax.fori_loop(half * steps, (half + 1) * steps, norm, grads)
    by_gain = jnp.sum(grads[0], axis=0, keepdims=True)
    by_head = lax.dot_general(
        grads[1], expand, (((1,), (1,)), ((), ())), preferred_element_type=F32, precision=HIGH
    )
    by_head = jnp.sum(by_head, axis=0, keepdims=True)
    for r in range(8):
        send_g[r : r + 1, :] = by_gain[:, r * BLK : (r + 1) * BLK]
    send_g[8:9, :] = jnp.zeros((1, BLK), F32)
    send_g[8:9, 0:16] = by_head

    def g_copy(dd, dy, dz, arriving):
        where = {"dp": lax.rem(dp + dd, 2), **at(dy, dz)}
        o = where["dp"] * 16 + where["ctx_0"] * 8 + where["ctx_1"]
        slot = o if arriving else me
        return pltpu.make_async_remote_copy(
            src_ref=send_g, dst_ref=recv_g.at[slot], send_sem=g_send.at[o], recv_sem=g_recv.at[slot],
            device_id=where, device_id_type=MESH,
        )

    for peer in ALL:
        g_copy(*peer, False).start()
    outputs[1].start()
    recv_g[me] = send_g[...]
    for peer in ALL:
        g_copy(*peer, True).wait_recv()
    summed = recv_g[0]
    for n in range(1, 32):
        summed = summed + recv_g[n]
    ggain_ref[...] = summed[0:8]
    gskip_ref[...] = summed[8:9, 0:16]

    for output in outputs:
        output.wait()
    for half in range(2):
        for d in range(4):
            ring(0, d, True, half).wait_send()
        for d in range(3):
            ring(0, d, False, half).wait_send()
    for zs in range(8):
        y_copy(zs, 0, True).wait_send()

        @pl.when(y == 1)
        def _():
            y_copy(zs, 1, True).wait_send()

    for dy, dz in PEERS:
        d_copy(dy, dz).wait_send()
        for half in range(2):
            s_copy(dy, dz, half).wait_send()
            e_copy(dy, dz, half).wait_send()
    for peer in ALL:
        g_copy(*peer, False).wait_send()


def hand_on(*refs):
    sources, results, held, (in_sem, out_sem) = refs[0:4], refs[4:8], refs[8:12], refs[12:]
    loads = [pltpu.make_async_copy(a, v, in_sem.at[n]) for n, (a, v) in enumerate(zip(sources, held))]
    stores = [pltpu.make_async_copy(v, a, out_sem.at[n]) for n, (v, a) in enumerate(zip(held, results))]
    for load in loads:
        load.start()
    for load, store in zip(loads, stores):
        load.wait()
        store.start()
    for store in stores:
        store.wait()


def body(
    queries, keys, values, doc_ids, inputs, gate_input, b_input, c_input, dt_raw, dt_bias, decay_log, skip, gain
):
    vmem = pl.BlockSpec(memory_space=pltpu.VMEM)
    dma = pltpu.SemaphoreType.DMA
    teacher, student, by_gain, by_skip = pl.pallas_call(
        kernel,
        out_shape=(
            jax.ShapeDtypeStruct((1, 256, 1024), BF16),
            jax.ShapeDtypeStruct((1, 256, 1024), BF16),
            jax.ShapeDtypeStruct((8, 128), F32),
            jax.ShapeDtypeStruct((1, 16), F32),
        ),
        in_specs=[pl.BlockSpec(memory_space=pl.ANY)] * 13,
        out_specs=(pl.BlockSpec(memory_space=pl.ANY),) * 2 + (vmem,) * 2,
        scratch_shapes=[
            pltpu.VMEM((1, 256, 1024), BF16),
            pltpu.VMEM((1, 256, 1024), BF16),
            pltpu.VMEM((1, 256, 1024), BF16),
            pltpu.VMEM((32, 128), jnp.int32),
            pltpu.VMEM((1, 256, 1024), BF16),
            pltpu.VMEM((1, 256, 1024), BF16),
            pltpu.VMEM((1, 256, 128), BF16),
            pltpu.VMEM((1, 256, 128), BF16),
            pltpu.VMEM((1, 16, 256), F32),
            pltpu.VMEM((1, 16), F32),
            pltpu.VMEM((1, 16), F32),
            pltpu.VMEM((1, 16), F32),
            pltpu.VMEM((1, 1024), F32),
            pltpu.VMEM((16, 2, 2, BLK, DH), BF16),
            pltpu.VMEM((2, DH, 1024), BF16),
            pltpu.VMEM((2, DH, 1024), F32),
            pltpu.VMEM((2, 1, 1024), F32),
            pltpu.VMEM((2, 1, 1024), F32),
            pltpu.VMEM((2, 8, BLK), F32),
            pltpu.VMEM((256, 1024), F32),
            pltpu.VMEM((256, 1024), F32),
            pltpu.VMEM((16, 2, 64, BLK), BF16),
            pltpu.VMEM((16, 2, 64, BLK), BF16),
            pltpu.VMEM((8, 2, BLK), F32),
            pltpu.VMEM((16, 2, BLK), F32),
            pltpu.VMEM((16, 2, 64, BLK), BF16),
            pltpu.VMEM((16, 2, 64, BLK), BF16),
            pltpu.VMEM((9, BLK), F32),
            pltpu.VMEM((32, 9, BLK), F32),
            dma((11,)), dma((2,)), dma((2, 2)), dma((2, 4, 2)), dma((16, 2)), dma((8, 2)), dma((8, 2)),
            dma((16, 2)), dma((16, 2)), dma((16,)), dma((16,)), dma((16, 2)), dma((16, 2)), dma((32,)), dma((32,)),
        ],
        compiler_params=pltpu.CompilerParams(
            collective_id=0, has_side_effects=True, vmem_limit_bytes=67043328
        ),
    )(
        queries, keys, values, doc_ids.reshape(32, 128), inputs, gate_input, b_input, c_input,
        dt_raw.transpose(0, 2, 1), dt_bias.reshape(1, 16), decay_log.reshape(1, 16), skip.reshape(1, 16),
        gain.reshape(1, 1024),
    )
    anywhere = pl.BlockSpec(memory_space=pl.ANY)
    results = (teacher, student, by_gain, by_skip)
    teacher, student, by_gain, by_skip = pl.pallas_call(
        hand_on,
        out_shape=tuple(jax.ShapeDtypeStruct(a.shape, a.dtype) for a in results),
        in_specs=[anywhere] * 4,
        out_specs=(anywhere,) * 4,
        scratch_shapes=[pltpu.VMEM(a.shape, a.dtype) for a in results] + [dma((4,)), dma((4,))],
        compiler_params=pltpu.CompilerParams(vmem_limit_bytes=67043328),
    )(*results)
    return teacher, student, by_gain.reshape(1024), by_skip.reshape(16)


def solution(mesh):
    split = Mesh(
        mesh.devices.reshape(mesh.shape["dp"], 2, 8, mesh.shape["head"]),
        ("dp", "ctx_0", "ctx_1", "head"),
    )
    rows = P("dp", CTX, "head")
    return jax.shard_map(
        body,
        mesh=split,
        in_specs=(rows, rows, rows, P("dp", None), rows, rows, rows, rows, rows)
        + (P("head"),) * 4,
        out_specs=(rows, rows, P("head"), P("head")),
        check_vma=False,
    )
```

time: 76.8 us -> 64.8 us (0.84); the launches traced: 75.9 us -> 64.7 us
  local copies, waits for them, and re-layouts: 9.03 us -> 0 us
  Pallas kernels: 66.1 us -> 64 us
    unnamed x29 -> x0, local copies, waits for them, and re-layouts: 9.03 us -> none
    pallas_call x1, Pallas kernels: 66.1 us -> 61.9 us  [body(): pl.pallas_call(kernel, out_shape=(jax.ShapeDtypeStruct((1, 256, 1024), BF...]
    pallas_call x0 -> x1, Pallas kernels: none -> 2.08 us  [body(): pl.pallas_call(hand_on, out_shape=tuple((jax.ShapeDtypeStruct(a.shape, a....]
where the time goes in v2:
time: 64.8 us; the launch traced here: 64.7 us
  Pallas kernels  64 us (99%)
    pallas_call x1, Pallas kernels, body(): pl.pallas_call(kernel, out_shape=(jax.ShapeDtypeStruct((1, 256, 1024), BF...  61.9 us
    pallas_call x1, Pallas kernels, body(): pl.pallas_call(hand_on, out_shape=tuple((jax.ShapeDtypeStruct(a.shape, a....  2.08 us

profile of v2, /device:TPU:4, one launch (start us, length us, event | category | flops | bytes accessed | tf_op | source)
XLA Modules:
  0.0 64.7 jit_solution(6746669949035984109)
XLA Ops:
  0.6 61.9 %shard_map.156 = (bf16[1,256,1024]{2,1,0:T(8,128)(2,1)}, bf16[1,256,1024]{2,1,0:T(8,128)(2,1)}, f32[8,128]{1,0:T(8,128)}, f32[1,16]{1,0:T(1,128)}) custom-call(bf16[1,256,1024]{2,1,0:T(8,128)(2,1)} %q_hbm.1, bf16[1,256,128]{2,1,0:T(8,128)(2,1)} %k_hbm.1, bf16[1,256,128]{2,1,0:T(8,128)(2,1)} %v_hbm.1, s32[32,128]{1,0:T(8,128)} %bitcast.8, ...), custom_call_target="tpu_custom_call" | custom-call | tf_op jit(solution)/shard_map/pallas_call | solution.py:482
  62.6 2.1 %shard_map.157 = (bf16[1,256,1024]{2,1,0:T(8,128)(2,1)}, bf16[1,256,1024]{2,1,0:T(8,128)(2,1)}, f32[8,128]{1,0:T(8,128)}, f32[1,16]{1,0:T(1,128)}) custom-call(bf16[1,256,1024]{2,1,0:T(8,128)(2,1)} %get-tuple-element.12.refs_0_, bf16[1,256,1024]{2,1,0:T(8,128)(2,1)} %get-tuple-element.13.refs_1_, f32[8,128]{1,0:T(8,128)} %get-tuple-element.14.refs_2_, ...), custom_call_target="tpu_custom_call" | custom-call | tf_op jit(solution)/shard_map/pallas_call | solution.py:535

commit v3 on v2

--- a/solution.py
+++ b/solution.py
@@ -10,8 +10,19 @@
 
 DH = 128
 BLK = 128
-PEERS = [(dy, dz) for dy in range(2) for dz in range(8) if (dy, dz) != (0, 0)]
-ALL = [(dd, dy, dz) for dd in range(2) for dy in range(2) for dz in range(8) if (dd, dy, dz) != (0, 0, 0)]
+
+
+def distance(dd, dy, dz):
+    return min(dz, 8 - dz) + (1 if dd else 2 * dy)
+
+
+PEERS = sorted(
+    [(dy, dz) for dy in range(2) for dz in range(8) if (dy, dz) != (0, 0)], key=lambda p: -distance(0, *p)
+)
+ALL = sorted(
+    [(dd, dy, dz) for dd in range(2) for dy in range(2) for dz in range(8) if (dd, dy, dz) != (0, 0, 0)],
+    key=lambda p: -distance(*p),
+)
 MESH = pl.DeviceIdType.MESH
 CTX = ("ctx_0", "ctx_1")
 F32 = jnp.float32
@@ -33,10 +44,10 @@
     q_hbm, k_hbm, v_hbm, docs_hbm, x_hbm, gate_hbm, b_hbm, c_hbm, dtr_hbm, bias_hbm, decay_hbm, skip_hbm, gain_hbm,
     teacher_hbm, student_hbm, ggain_ref, gskip_ref,
     teacher_ref, student_ref, q_ref, docs_ref, x_ref, gate_ref, b_ref, c_ref, dtr_ref, bias_ref, decay_ref, skip_ref, gain_ref,
-    kv, qt, acc, top, total, doc_start, mixed, reach_wide,
+    silu_ref, kv, qt, acc, top, total, doc_start, mixed, reach_wide,
     send_s, recv_s, send_d, recv_d, send_e, recv_e, send_g, recv_g,
     in_sem, out_sem, kv_sem, ring_send, ring_recv, y_send, y_recv,
-    s_send, s_recv, d_send, d_recv, e_send, e_recv, g_send, g_recv,
+    s_send, s_recv, d_send, d_recv, e_send, e_recv, g_send, g_recv, ready,
 ):
     dp = lax.axis_index("dp")
     y = lax.axis_index("ctx_0")
@@ -53,9 +64,10 @@
         return {"ctx_0": lax.rem(y + dy, 2), "ctx_1": zmod(z + dz)}
 
     barrier = pltpu.get_barrier_semaphore()
-    for dd, dy, dz in ALL:
-        where = {"dp": lax.rem(dp + dd, 2), **at(dy, dz)}
-        pl.semaphore_signal(barrier, inc=1, device_id=where, device_id_type=MESH)
+    for dy, dz in PEERS:
+        pl.semaphore_signal(barrier, inc=1, device_id=at(dy, dz), device_id_type=MESH)
+    partner = {"dp": 1 - dp}
+    pl.semaphore_signal(barrier, inc=1, device_id=partner, device_id_type=MESH)
 
     arrays = (
         (docs_hbm, docs_ref), (dtr_hbm, dtr_ref), (bias_hbm, bias_ref), (decay_hbm, decay_ref),
@@ -216,21 +228,22 @@
             device_id=other, device_id_type=MESH,
         )
 
-    rest = local_terms(0)
+    rests = [local_terms(half) for half in range(2)]
     for load in kv_loads:
         load.wait()
-    pl.semaphore_wait(barrier, len(ALL))
-
+    pl.semaphore_wait(barrier, len(PEERS) + 1)
+    pl.semaphore_signal(ready, inc=1, device_id=partner, device_id_type=MESH)
     for half in range(2):
         ring(0, 0, True, half).start()
         ring(0, 0, False, half).start()
         y_start(z, half)
-    for dy, dz in PEERS:
+    for dy, dz in PEERS[:8]:
+        d_copy(dy, dz).start()
         s_copy(dy, dz, 0).start()
-    rest()
-    rest = local_terms(1)
     recv_s[b] = send_s[b]
     recv_d[b] = send_d[z]
+    for rest in rests:
+        rest()
 
     loads[8].wait()
     for half in range(2):
@@ -311,16 +324,20 @@
                 ids.append(theirs(source(off)))
         sources(ids)
 
-    hop(1)
-    for dy, dz in PEERS:
-        d_copy(dy, dz).start()
-        s_copy(dy, dz, 1).start()
-    rest()
     item(b, 0, 0, True)
     item(b, 1, 1, True)
     item(b, 0, 1, False)
+
+    hop(1)
+    for dy, dz in PEERS[8:]:
+        d_copy(dy, dz).start()
+        s_copy(dy, dz, 0).start()
+    hop(2)
+    for dy, dz in PEERS:
+        s_copy(dy, dz, 1).start()
     attend(1)
-    hop(2)
+    hop(3)
+    attend(2)
 
     def s_wait(k, half):
         @pl.when(k != b)
@@ -350,25 +367,30 @@
         return state
 
     state = scan(0, jnp.zeros((64, BLK), F32))
-    attend(2)
-    hop(3)
-    scan(1, state)
     attend(3)
     hop(4)
+    scan(1, state)
+    for load in loads[9:]:
+        load.wait()
+
+    def activate(i, carry):
+        rows = pl.ds(pl.multiple_of(i * 16, 16), 16)
+        gate = gate_ref[0, rows, :].astype(F32)
+        silu_ref[rows, :] = gate / (1.0 + jnp.exp(-gate))
+        return carry
+
+    lax.fori_loop(0, 16, activate, 0)
     attend(4)
     y_arrived(source(-way * 4))
     other_source(theirs(source(-way * 4)))
 
-    for load in loads[9:]:
-        load.wait()
     gain = gain_ref[...]
     rows_at_once = 16
 
     def norm(i, carry):
         by_gain, by_skip = carry
         rows = pl.ds(pl.multiple_of(i * rows_at_once, rows_at_once), rows_at_once)
-        gate = gate_ref[0, rows, :].astype(F32)
-        silu = gate / (1.0 + jnp.exp(-gate))
+        silu = silu_ref[rows, :]
         gated = mixed[rows, :] * silu
         mean = jnp.sum(gated * gated, axis=1, keepdims=True) * (1.0 / 1024)
         inv = lax.rsqrt(mean + 1e-05)
@@ -426,6 +448,7 @@
             device_id=where, device_id_type=MESH,
         )
 
+    pl.semaphore_wait(ready, 1)
     for peer in ALL:
         g_copy(*peer, False).start()
     outputs[1].start()
@@ -503,6 +526,7 @@
             pltpu.VMEM((1, 16), F32),
             pltpu.VMEM((1, 16), F32),
             pltpu.VMEM((1, 1024), F32),
+            pltpu.VMEM((256, 1024), F32),
             pltpu.VMEM((16, 2, 2, BLK, DH), BF16),
             pltpu.VMEM((2, DH, 1024), BF16),
             pltpu.VMEM((2, DH, 1024), F32),
@@ -520,7 +544,7 @@
             pltpu.VMEM((9, BLK), F32),
             pltpu.VMEM((32, 9, BLK), F32),
             dma((11,)), dma((2,)), dma((2, 2)), dma((2, 4, 2)), dma((16, 2)), dma((8, 2)), dma((8, 2)),
-            dma((16, 2)), dma((16, 2)), dma((16,)), dma((16,)), dma((16, 2)), dma((16, 2)), dma((32,)), dma((32,)),
+            dma((16, 2)), dma((16, 2)), dma((16,)), dma((16,)), dma((16, 2)), dma((16, 2)), dma((32,)), dma((32,)), pltpu.SemaphoreType.REGULAR,
         ],
         compiler_params=pltpu.CompilerParams(
             collective_id=0, has_side_effects=True, vmem_limit_bytes=67043328

time: 64.8 us -> 62.1 us (0.958)
  Pallas kernels: 64 us -> 61.3 us
    pallas_call x1, Pallas kernels: 61.9 us -> 59.2 us  [body(): pl.pallas_call(kernel, out_shape=(jax.ShapeDtypeStruct((1, 256, 1024), BF...]
where the time goes in v3:
time: 62.1 us; the launch traced here: 61.9 us
  Pallas kernels  61.3 us (99%)
  between operations  0.64 us (1%)
    pallas_call x1, Pallas kernels, body(): pl.pallas_call(kernel, out_shape=(jax.ShapeDtypeStruct((1, 256, 1024), BF...  59.2 us
    pallas_call x1, Pallas kernels, body(): pl.pallas_call(hand_on, out_shape=tuple((jax.ShapeDtypeStruct(a.shape, a....  2.08 us

profile of v3, /device:TPU:4, one launch (start us, length us, event | category | flops | bytes accessed | tf_op | source)
XLA Modules:
  0.0 61.9 jit_solution(16724097967883241962)
XLA Ops:
  0.6 59.2 %shard_map.156 = (bf16[1,256,1024]{2,1,0:T(8,128)(2,1)}, bf16[1,256,1024]{2,1,0:T(8,128)(2,1)}, f32[8,128]{1,0:T(8,128)}, f32[1,16]{1,0:T(1,128)}) custom-call(bf16[1,256,1024]{2,1,0:T(8,128)(2,1)} %q_hbm.1, bf16[1,256,128]{2,1,0:T(8,128)(2,1)} %k_hbm.1, bf16[1,256,128]{2,1,0:T(8,128)(2,1)} %v_hbm.1, s32[32,128]{1,0:T(8,128)} %bitcast.8, ...), custom_call_target="tpu_custom_call" | custom-call | tf_op jit(solution)/shard_map/pallas_call | solution.py:505
  59.8 2.1 %shard_map.157 = (bf16[1,256,1024]{2,1,0:T(8,128)(2,1)}, bf16[1,256,1024]{2,1,0:T(8,128)(2,1)}, f32[8,128]{1,0:T(8,128)}, f32[1,16]{1,0:T(1,128)}) custom-call(bf16[1,256,1024]{2,1,0:T(8,128)(2,1)} %get-tuple-element.12.refs_0_, bf16[1,256,1024]{2,1,0:T(8,128)(2,1)} %get-tuple-element.13.refs_1_, f32[8,128]{1,0:T(8,128)} %get-tuple-element.14.refs_2_, ...), custom_call_target="tpu_custom_call" | custom-call | tf_op jit(solution)/shard_map/pallas_call | solution.py:559

commit v4 on v3

--- a/solution.py
+++ b/solution.py
@@ -176,6 +176,31 @@
             device_id={"ctx_1": zmod(z + (way if forward else -way))}, device_id_type=MESH,
         )
 
+    def wanted(zs, forward, gone):
+        sign = way if forward else -way
+        some = y == 1
+        for k in range(gone + 1, 5 if forward else 4):
+            some = some | (zmod(zs + sign * k) < zs)
+        return some
+
+    def ring_start(off, dist, forward, half):
+        if half == 0:
+            ring(off, dist, forward, 0).start()
+        else:
+
+            @pl.when(wanted(source(off), forward, dist))
+            def _():
+                ring(off, dist, forward, 1).start()
+
+    def ring_arrived(off, dist, forward, half):
+        if half == 0:
+            ring(off, 0, forward, 0).wait_recv()
+        else:
+
+            @pl.when(wanted(source(off), forward, dist - 1))
+            def _():
+                ring(off, 0, forward, 1).wait_recv()
+
     def y_copy(zs, half, mine):
         s = (y if mine else 1 - y) * 8 + zs
         return pltpu.make_async_remote_copy(
@@ -228,20 +253,18 @@
             device_id=other, device_id_type=MESH,
         )
 
-    rests = [local_terms(half) for half in range(2)]
+    rests = [local_terms(0)]
     for load in kv_loads:
         load.wait()
     pl.semaphore_wait(barrier, len(PEERS) + 1)
     pl.semaphore_signal(ready, inc=1, device_id=partner, device_id_type=MESH)
     for half in range(2):
-        ring(0, 0, True, half).start()
-        ring(0, 0, False, half).start()
+        ring_start(0, 0, True, half)
+        ring_start(0, 0, False, half)
         y_start(z, half)
     for dy, dz in PEERS[:8]:
-        d_copy(dy, dz).start()
         s_copy(dy, dz, 0).start()
-    recv_s[b] = send_s[b]
-    recv_d[b] = send_d[z]
+    rests.append(local_terms(1))
     for rest in rests:
         rest()
 
@@ -301,14 +324,14 @@
         up = source(-way * d)
         down = source(way * d)
         for half in range(2):
-            ring(-way * d, 0, True, half).wait_recv()
+            ring_arrived(-way * d, d, True, half)
             if d < 4:
-                ring(-way * d, d, True, half).start()
+                ring_start(-way * d, d, True, half)
             y_start(up, half)
             if d < 4:
-                ring(way * d, 0, False, half).wait_recv()
+                ring_arrived(way * d, d, False, half)
                 if d < 3:
-                    ring(way * d, d, False, half).start()
+                    ring_start(way * d, d, False, half)
                 y_start(down, half)
 
     def attend(d):
@@ -329,8 +352,11 @@
     item(b, 0, 1, False)
 
     hop(1)
+    recv_s[b] = send_s[b]
+    recv_d[b] = send_d[z]
+    for dy, dz in PEERS:
+        d_copy(dy, dz).start()
     for dy, dz in PEERS[8:]:
-        d_copy(dy, dz).start()
         s_copy(dy, dz, 0).start()
     hop(2)
     for dy, dz in PEERS:
@@ -463,11 +489,20 @@
 
     for output in outputs:
         output.wait()
-    for half in range(2):
-        for d in range(4):
-            ring(0, d, True, half).wait_send()
-        for d in range(3):
-            ring(0, d, False, half).wait_send()
+    for d in range(4):
+        ring(0, d, True, 0).wait_send()
+
+        @pl.when(wanted(source(-way * d), True, d))
+        def _():
+            ring(0, d, True, 1).wait_send()
+
+    for d in range(3):
+        ring(0, d, False, 0).wait_send()
+
+        @pl.when(wanted(source(way * d), False, d))
+        def _():
+            ring(0, d, False, 1).wait_send()
+
     for zs in range(8):
         y_copy(zs, 0, True).wait_send()
 

time: 62.1 us -> 61.8 us (level)
  no operation moved by 1% of the time
where the time goes in v4:
time: 61.8 us; the launch traced here: 61.7 us
  Pallas kernels  61 us (99%)
  between operations  0.64 us (1%)
    pallas_call x1, Pallas kernels, body(): pl.pallas_call(kernel, out_shape=(jax.ShapeDtypeStruct((1, 256, 1024), BF...  59 us
    pallas_call x1, Pallas kernels, body(): pl.pallas_call(hand_on, out_shape=tuple((jax.ShapeDtypeStruct(a.shape, a....  2.08 us

profile of v4, /device:TPU:4, one launch (start us, length us, event | category | flops | bytes accessed | tf_op | source)
XLA Modules:
  0.0 61.7 jit_solution(7225388217098763391)
XLA Ops:
  0.6 59.0 %shard_map.156 = (bf16[1,256,1024]{2,1,0:T(8,128)(2,1)}, bf16[1,256,1024]{2,1,0:T(8,128)(2,1)}, f32[8,128]{1,0:T(8,128)}, f32[1,16]{1,0:T(1,128)}) custom-call(bf16[1,256,1024]{2,1,0:T(8,128)(2,1)} %q_hbm.1, bf16[1,256,128]{2,1,0:T(8,128)(2,1)} %k_hbm.1, bf16[1,256,128]{2,1,0:T(8,128)(2,1)} %v_hbm.1, s32[32,128]{1,0:T(8,128)} %bitcast.8, ...), custom_call_target="tpu_custom_call" | custom-call | tf_op jit(solution)/shard_map/pallas_call | solution.py:540
  59.6 2.1 %shard_map.157 = (bf16[1,256,1024]{2,1,0:T(8,128)(2,1)}, bf16[1,256,1024]{2,1,0:T(8,128)(2,1)}, f32[8,128]{1,0:T(8,128)}, f32[1,16]{1,0:T(1,128)}) custom-call(bf16[1,256,1024]{2,1,0:T(8,128)(2,1)} %get-tuple-element.12.refs_0_, bf16[1,256,1024]{2,1,0:T(8,128)(2,1)} %get-tuple-element.13.refs_1_, f32[8,128]{1,0:T(8,128)} %get-tuple-element.14.refs_2_, ...), custom_call_target="tpu_custom_call" | custom-call | tf_op jit(solution)/shard_map/pallas_call | solution.py:594
